TPU v7x, 256 devices: a whole 4x4x8 slice. The times are simulated.
256 devices in a mesh: dp: 64 (over z, x, core), mp: 4 (over y).
Axes of the slice: x: 4, y: 4, z: 8, core: 2. Of those that a mesh axis runs over, the one named last changes fastest.
Arguments:
- tokens: bfloat16 [32768, 8192], P('dp', 'mp'), may hold values from -6 to 6
- base_weight: bfloat16 [8192, 1024], P('mp'), may hold values from -0.0625 to 0.0625
- adapter_down: bfloat16 [256, 32, 8192], P('dp', None, 'mp'), may hold values from -0.0625 to 0.0625
- adapter_up: bfloat16 [256, 32, 1024], P('dp', None, 'mp'), may hold values from -1 to 1
- block_adapter: int32 [1024], P('dp'), may hold values from 0 to 255, as said below
- cotangent: bfloat16 [32768, 1024], P('dp', 'mp'), may hold values from -6 to 6
Outputs:
- output: bfloat16 [32768, 1024], P('dp', 'mp')
- input_grad: bfloat16 [32768, 8192], P('dp', 'mp')
- down_grad: float32 [256, 32, 8192], P('dp', None, 'mp')
- up_grad: float32 [256, 32, 1024], P('dp', None, 'mp')
Inputs may be any that keep to these rules, and one draw needn't show every extreme that they name: `block_adapter`: adapter a is owned by index a // 4 of dp; the 16 blocks of one index of dp name adapters of 16 different owners.
All inputs are finite; a program needn't handle non-finite values.
Results may differ from a plain program's by a relative error of at most 0.0045.
Values may be sent and summed in bfloat16 or wider, within the bound.
No kernel may reach another device: no remote copies, remote signals or barrier semaphores. Data moves between devices by JAX's collectives and lax.ppermute only.
A program may use at most 128 MiB of HBM per device.

v0:
```python
import functools

import jax
import jax.numpy as jnp
from jax import lax
from jax.experimental import pallas as pl
from jax.experimental.pallas import tpu as pltpu
from jax.sharding import Mesh, PartitionSpec as P

adapter_scale = 2.0
PLANE = 8
QUAD = 4
f32, bf = jnp.float32, jnp.bfloat16

SMEM = functools.partial(pl.BlockSpec, memory_space=pltpu.SMEM)
VMEM = functools.partial(pl.BlockSpec, memory_space=pltpu.VMEM)


def diagonal(length, rank):
    rows = lax.broadcasted_iota(jnp.int32, (QUAD * length, QUAD * rank), 0) // length
    cols = lax.broadcasted_iota(jnp.int32, (QUAD * length, QUAD * rank), 1) // rank
    return rows == cols


def fold(product, mask, length):
    kept = jnp.where(mask, product, 0.0)
    total = kept[:length]
    for i in range(1, QUAD):
        total = total + kept[i * length : (i + 1) * length]
    return total


def spread(quad, mask):
    wide = jnp.concatenate([quad] * QUAD, axis=0)
    return jnp.where(mask, wide, jnp.zeros_like(wide))


def dot_nt(a, b):
    return lax.dot_general(a, b, (((1,), (1,)), ((), ())), preferred_element_type=f32)


def dot_nn(a, b):
    return lax.dot_general(a, b, (((1,), (0,)), ((), ())), preferred_element_type=f32)


def dot_tn(a, b):
    return lax.dot_general(a, b, (((0,), (0,)), ((), ())), preferred_element_type=f32)


HBM = functools.partial(pl.BlockSpec, memory_space=pl.ANY)


def stacked(count, like):
    return [pltpu.VMEM((count,) + like.shape, like.dtype), pltpu.SemaphoreType.DMA((count,))]


def load(refs, stack, sems):
    for k, ref in enumerate(refs):
        pltpu.make_async_copy(ref, stack.at[k], sems.at[k]).start()


def loaded(refs, stack, sems, k):
    pltpu.make_async_copy(refs[0], stack.at[k], sems.at[k]).wait()


def back(me, k, size):
    return lax.rem(me - k + size, size)


def select_up(ids_all, me, gathered, plane):
    planes, owned, rank, cols = gathered.shape
    blocks = ids_all.shape[0] // plane

    def kernel(ids_ref, me_ref, all_ref, out_ref):
        my_g = me_ref[1]

        def step(b, carry):
            number = ids_ref[b]
            owner = lax.div(number, owned)

            @pl.when(lax.rem(owner, plane) == my_g)
            def _():
                z = lax.div(owner, plane)
                out_ref[lax.div(b, blocks), z] = all_ref[z, lax.rem(number, owned)]

            return carry

        lax.fori_loop(0, plane * blocks, step, 0, unroll=4)

    return pl.pallas_call(
        kernel,
        in_specs=[SMEM(), SMEM(), VMEM()],
        out_specs=VMEM(),
        out_shape=jax.ShapeDtypeStruct((plane, planes, rank, cols), bf),
        name="select_up",
    )(ids_all, me, gathered)


def up_rows(ids_ref, slots_ref, q, owned, plane):
    rows = []
    for i in range(QUAD):
        owner = ids_ref[q * QUAD + i] // owned
        rows.append(slots_ref[owner % plane, owner // plane])
    return jnp.concatenate(rows, axis=0)


def rank_grad_part(ids, slots, cot, owned):
    plane, _, rank, _ = slots.shape
    blocks = ids.shape[0]
    length = cot.shape[0] // blocks
    quads = blocks // QUAD
    span = QUAD * length

    def kernel(ids_ref, slots_ref, cot_ref, out_ref):
        mask = diagonal(length, rank)
        for q in range(quads):
            up = up_rows(ids_ref, slots_ref, q, owned, plane)
            out_ref[q] = fold(dot_nt(cot_ref[q * span : (q + 1) * span, :], up), mask, length)

    return pl.pallas_call(
        kernel,
        in_specs=[SMEM(), VMEM(), VMEM()],
        out_specs=VMEM(),
        out_shape=jax.ShapeDtypeStruct((quads, length, QUAD * rank), f32),
        name="rank_grad_part",
    )(ids, slots, cot)


def down_terms(ids_all, me, rg, tok, adapters, rank):
    plane = len(rg)
    quads, length = rg[0].shape[:2]
    span = QUAD * length
    blocks = quads * QUAD
    narrow = tok[0].shape[1]

    def kernel(ids_ref, me_ref, *refs):
        rgs, toks = refs[:plane], refs[plane : 2 * plane]
        out_ref, acc, rg_stack, rg_sems, tok_stack, tok_sems = refs[2 * plane :]
        mask = diagonal(length, rank)
        load(rgs, rg_stack, rg_sems)
        load(toks, tok_stack, tok_sems)

        def clear(c, carry):
            acc[pl.ds(c * 8, 8)] = jnp.zeros((8, rank, narrow), f32)
            return carry

        lax.fori_loop(0, adapters // 8, clear, 0)

        def step(k, carry):
            loaded(rgs, rg_stack, rg_sems, k)
            loaded(toks, tok_stack, tok_sems, k)
            src = back(me_ref[1], k, plane)
            for q in range(quads):
                wide = spread(rg_stack[k, q], mask)
                rows = tok_stack[k, q * span : (q + 1) * span, :]
                got = dot_tn(wide, rows) * (1.0 / length)
                for i in range(QUAD):
                    a = ids_ref[src * blocks + q * QUAD + i]
                    acc[a] = acc[a] + got[i * rank : (i + 1) * rank]
            return carry

        lax.fori_loop(0, plane, step, 0)

        def finish(c, carry):
            out_ref[pl.ds(c * 8, 8)] = acc[pl.ds(c * 8, 8)].astype(bf)
            return carry

        lax.fori_loop(0, adapters // 8, finish, 0)

    return pl.pallas_call(
        kernel,
        in_specs=[SMEM(), SMEM()] + [HBM()] * (2 * plane),
        out_specs=VMEM(),
        out_shape=jax.ShapeDtypeStruct((adapters, rank, narrow), bf),
        scratch_shapes=[pltpu.VMEM((adapters, rank, narrow), f32)]
        + stacked(plane, rg[0])
        + stacked(plane, tok[0]),
        name="down_terms",
    )(ids_all, me, *rg, *tok)


def table_rows(ids_ref, table_ref, first):
    return jnp.concatenate([table_ref[ids_ref[first + i]] for i in range(QUAD)], axis=0)


def rank_part(ids_all, me, table, tok):
    plane = len(tok)
    tokens, _ = tok[0].shape
    rank = table.shape[1]
    blocks = ids_all.shape[0] // plane
    length = tokens // blocks
    quads = blocks // QUAD
    span = QUAD * length

    def kernel(ids_ref, me_ref, table_ref, *refs):
        toks, (out_ref, stack, sems) = refs[:plane], refs[plane:]
        mask = diagonal(length, rank)
        load(toks, stack, sems)

        def step(k, carry):
            dest = back(me_ref[1], k, plane)
            loaded(toks, stack, sems, k)
            for q in range(quads):
                down = table_rows(ids_ref, table_ref, dest * blocks + q * QUAD)
                got = dot_nt(stack[k, q * span : (q + 1) * span, :], down)
                out_ref[dest, q] = fold(got, mask, length)
            return carry

        lax.fori_loop(0, plane, step, 0)

    return pl.pallas_call(
        kernel,
        in_specs=[SMEM(), SMEM(), VMEM()] + [HBM()] * plane,
        out_specs=VMEM(),
        out_shape=jax.ShapeDtypeStruct((plane, quads, length, QUAD * rank), f32),
        scratch_shapes=stacked(plane, tok[0]),
        name="rank_part",
    )(ids_all, me, table, *tok)


def through_down(ids_all, me, table, rg):
    plane = len(rg)
    quads, length = rg[0].shape[:2]
    rank, narrow = table.shape[1:]
    span = QUAD * length
    blocks = quads * QUAD
    piece = jax.ShapeDtypeStruct((quads * span, narrow), bf)

    def kernel(ids_ref, me_ref, table_ref, *refs):
        rgs, outs = refs[:plane], refs[plane : 2 * plane]
        rg_stack, rg_sems, stack, sems = refs[2 * plane :]
        mask = diagonal(length, rank)
        load(rgs, rg_stack, rg_sems)

        def step(k, carry):
            loaded(rgs, rg_stack, rg_sems, k)
            src = back(me_ref[1], k, plane)
            for q in range(quads):
                down = table_rows(ids_ref, table_ref, src * blocks + q * QUAD)
                got = dot_nn(spread(rg_stack[k, q], mask), down)
                stack[k, q * span : (q + 1) * span, :] = got.astype(bf)
            return carry

        lax.fori_loop(0, plane, step, 0)
        for k in range(plane):
            pltpu.make_async_copy(stack.at[k], outs[k], sems.at[k]).start()
        for k in range(plane):
            pltpu.make_async_copy(stack.at[k], outs[k], sems.at[k]).wait()

    return pl.pallas_call(
        kernel,
        in_specs=[SMEM(), SMEM(), VMEM()] + [HBM()] * plane,
        out_specs=tuple([HBM()] * plane),
        out_shape=tuple([piece] * plane),
        scratch_shapes=stacked(plane, rg[0]) + stacked(plane, piece),
        name="through_down",
    )(ids_all, me, table, *rg)


def output_and_up(ids, ranks, slots, cot, base, owned):
    plane, _, rank, _ = slots.shape
    quads, length = ranks.shape[:2]
    span = QUAD * length

    def kernel(ids_ref, rank_ref, slots_ref, cot_ref, base_ref, out_ref, send_ref):
        mask = diagonal(length, rank)
        for q in range(quads):
            wide = spread(rank_ref[q], mask)
            up = up_rows(ids_ref, slots_ref, q, owned, plane)
            rows = slice(q * span, (q + 1) * span)
            out_ref[rows, :] = (base_ref[rows, :] + adapter_scale * dot_nn(wide, up)).astype(bf)
            got = (dot_tn(wide, cot_ref[rows, :]) * (adapter_scale / length)).astype(bf)
            for i in range(QUAD):
                owner = ids_ref[q * QUAD + i] // owned
                send_ref[owner % plane, owner // plane] = got[i * rank : (i + 1) * rank]

    return pl.pallas_call(
        kernel,
        in_specs=[SMEM()] + [VMEM()] * 4,
        out_specs=(VMEM(), VMEM()),
        out_shape=(
            jax.ShapeDtypeStruct(cot.shape, bf),
            jax.ShapeDtypeStruct(slots.shape, bf),
        ),
        name="output_and_up",
    )(ids, ranks, slots, cot, base)


def gather_up(ids_all, me, got, owned):
    plane, planes, rank, cols = got.shape
    blocks = ids_all.shape[0] // plane

    def kernel(ids_ref, me_ref, got_ref, *refs):
        outs, acc = refs[:planes], refs[planes]
        my_z, my_g = me_ref[0], me_ref[1]
        acc[...] = jnp.zeros(acc.shape, f32)

        def step(b, carry):
            number = ids_ref[b]
            owner = lax.div(number, owned)

            @pl.when(lax.rem(owner, plane) == my_g)
            def _():
                z, local = lax.div(owner, plane), lax.rem(number, owned)
                acc[z, local] = acc[z, local] + got_ref[lax.div(b, blocks), z].astype(f32)

            return carry

        lax.fori_loop(0, plane * blocks, step, 0, unroll=4)
        for k in range(planes):
            outs[k][...] = acc[lax.rem(my_z + k, planes)].astype(outs[k].dtype)

    chunk = (owned, rank, cols)
    return pl.pallas_call(
        kernel,
        in_specs=[SMEM(), SMEM(), VMEM()],
        out_specs=tuple([VMEM()] * planes),
        out_shape=tuple(jax.ShapeDtypeStruct(chunk, bf if k else f32) for k in range(planes)),
        scratch_shapes=[pltpu.VMEM((planes,) + chunk, f32)],
        name="gather_up",
    )(ids_all, me, got)


def base_gradient(me, cots, weight):
    parts = len(cots)
    tokens, cols = cots[0].shape
    features = weight.shape[0]
    tile = 256

    def kernel(me_ref, *refs):
        w_ref, out_ref = refs[parts], refs[parts + 1]
        total = jnp.zeros((tokens, tile), f32)
        for k in range(parts):
            first = pl.multiple_of(back(me_ref[2], k, parts) * cols, cols)
            total = total + dot_nt(refs[k][...], w_ref[:, pl.ds(first, cols)])
        out_ref[...] = total

    return pl.pallas_call(
        kernel,
        grid=(features // tile,),
        in_specs=[SMEM()]
        + [pl.BlockSpec((tokens, cols), lambda s: (0, 0))] * parts
        + [pl.BlockSpec((tile, parts * cols), lambda s: (s, 0))],
        out_specs=pl.BlockSpec((tokens, tile), lambda s: (0, s)),
        out_shape=jax.ShapeDtypeStruct((tokens, features), f32),
        name="base_gradient",
    )(me, *cots, weight)


def input_gradient(me, base, through):
    plane = len(through)
    tokens, narrow = through[0].shape

    def kernel(me_ref, base_ref, *refs):
        out_ref = refs[plane]
        for k in range(plane):
            first = pl.multiple_of(lax.rem(me_ref[1] + k, plane) * narrow, narrow)
            cols = pl.ds(first, narrow)
            out_ref[:, cols] = (base_ref[:, cols] + refs[k][...].astype(f32)).astype(bf)

    return pl.pallas_call(
        kernel,
        in_specs=[SMEM()] + [VMEM()] * (plane + 1),
        out_specs=VMEM(),
        out_shape=jax.ShapeDtypeStruct((tokens, plane * narrow), bf),
        name="input_gradient",
    )(me, base, *through)


def shift(x, axis, size, k):
    return lax.ppermute(x, axis, [(i, (i + k) % size) for i in range(size)])


def step(tokens, base_weight, adapter_down, adapter_up, block_adapter, cotangent):
    blocks = block_adapter.shape[0]
    owned, rank, width_local = adapter_down.shape
    _, local_columns = cotangent.shape
    planes, plane, parts = lax.axis_size("z"), lax.axis_size("g"), lax.axis_size("mp")
    my_mp = lax.axis_index("mp")
    my_g = lax.axis_index("g")
    me = jnp.stack([lax.axis_index("z"), my_g, my_mp]).astype(jnp.int32)
    adapters = planes * plane * owned
    narrow = width_local // plane

    def exchange(x, axis="g"):
        return lax.all_to_all(x, axis, split_axis=0, concat_axis=0, tiled=True)

    def sliced(x):
        return x.reshape(owned, rank, plane, narrow).transpose(2, 0, 1, 3)

    def mp_sum(x):
        total = x
        for k in range(1, parts):
            total = total + shift(x, "mp", parts, k)
        return total

    ids = block_adapter
    up_all = lax.all_gather(adapter_up, "z", axis=0)
    tile = jnp.pad(ids.astype(bf)[None, None], ((0, 0), (0, 15), (0, narrow - blocks)))
    sent = jnp.concatenate(
        [sliced(adapter_down).reshape(plane, owned * rank, narrow)]
        + [jnp.broadcast_to(tile, (plane, 16, narrow))],
        axis=1,
    )
    got = exchange(sent)
    ids_all = got[:, owned * rank, :blocks].astype(jnp.int32).reshape(-1)
    down_n = got[:, : owned * rank].reshape(plane * owned, rank, narrow)
    table = lax.all_gather(down_n, "z", axis=0, tiled=True)
    tok_n = []
    for k in range(plane):
        first = lax.rem(my_g + k, plane) * narrow
        part = lax.dynamic_slice_in_dim(tokens, first, narrow, axis=1)
        tok_n.append(shift(part, "g", plane, k) if k else part)
    cots = [cotangent] + [shift(cotangent, "mp", parts, k) for k in range(1, parts)]
    base_grad = base_gradient(me, cots, base_weight)
    base_part = jnp.dot(tokens, base_weight, preferred_element_type=f32)

    def columns(k):
        start = lax.rem(my_mp + k, parts) * local_columns
        return lax.dynamic_slice_in_dim(base_part, start, local_columns, axis=1)

    frozen = columns(0)
    for k in range(1, parts):
        frozen = frozen + shift(columns(k).astype(bf), "mp", parts, k).astype(f32)

    selected = select_up(ids_all, me, up_all, plane)
    slots = exchange(selected)
    rg_part = rank_grad_part(ids, slots, cotangent, owned)
    rg = (adapter_scale * mp_sum(rg_part)).astype(bf)
    rg_all = [rg] + [shift(rg, "g", plane, k) for k in range(1, plane)]

    part = rank_part(ids_all, me, table, tok_n)
    rank_parts = exchange(part)
    grad_table = down_terms(ids_all, me, rg_all, tok_n, adapters, rank)
    grad_n = lax.psum_scatter(grad_table, "z", scatter_dimension=0, tiled=True)
    grad_got = exchange(grad_n.reshape(plane, owned, rank, narrow))
    down_grad = jnp.concatenate([grad_got[i] for i in range(plane)], axis=-1).astype(f32)

    ranks = mp_sum(jnp.sum(rank_parts, axis=0)).astype(bf)

    through_n = through_down(ids_all, me, table, rg_all)
    through = [through_n[0]]
    through += [shift(through_n[k], "g", plane, plane - k) for k in range(1, plane)]
    input_grad = input_gradient(me, base_grad, through)

    output, up_send = output_and_up(ids, ranks, slots, cotangent, frozen, owned)
    up_got = exchange(up_send)
    up_chunks = gather_up(ids_all, me, up_got, owned)
    up_grad = up_chunks[0]
    for k in range(1, planes):
        up_grad = up_grad + shift(up_chunks[k], "z", planes, k).astype(f32)
    return (output, input_grad, down_grad, up_grad)


def solution(mesh):
    fine = Mesh(mesh.devices.reshape(-1, PLANE, mesh.devices.shape[1]), ("z", "g", "mp"))
    dp = ("z", "g")
    return jax.shard_map(
        step,
        mesh=fine,
        in_specs=(
            P(dp, "mp"),
            P("mp", None),
            P(dp, None, "mp"),
            P(dp, None, "mp"),
            P(dp),
            P(dp, "mp"),
        ),
        out_specs=(P(dp, "mp"), P(dp, "mp"), P(dp, None, "mp"), P(dp, None, "mp")),
        check_vma=False,
    )
```

profile of v0, /device:TPU:37, one launch (start us, length us, event | category | flops | bytes accessed | tf_op | source)
XLA Modules:
  0.0 257.3 jit_solution(6852982319602331307)
XLA Ops:
  9.1 13.0 %all_to_all.25 = bf16[8,144,256]{2,1,0:T(8,128)(2,1)S(1)} all-to-all(bf16[8,144,256]{2,1,0:T(8,128)(2,1)S(1)} %pad_maximum_fusion), channel_id=1, replica_groups=mesh['z'=8,'g'=8,'mp'=4] {'g'}, dimensions={0} | all-to-all | bytes 1179648 | tf_op jit(solution)/shard_map/all_to_all | solution.py:386
  23.6 26.6 %all-gather = bf16[32,32,256]{2,1,0:T(8,128)(2,1)} all-gather(bf16[4,32,256]{2,1,0:T(8,128)(2,1)S(1)} %copy-done.25), channel_id=2, replica_groups=mesh['z'=8,'g'=8,'mp'=4] {'z'}, dimensions={0}, use_global_device_ids=true | all-gather | bytes 589824 | tf_op jit(solution)/shard_map/all_gather | solution.py:398
  50.8 4.1 %select_up.1 = bf16[8,8,32,256]{3,2,1,0:T(8,128)(2,1)} custom-call(s32[128]{0:T(128)} %reshape.28.ids_ref, s32[3]{0:T(128)} %pad_add_fusion.me_ref, bf16[8,4,32,256]{3,2,1,0:T(8,128)(2,1)} %bitcast.53), custom_call_target="tpu_custom_call" | custom-call | tf_op jit(solution)/shard_map/select_up/pallas_call | solution.py:90
  54.9 11.7 %all-to-all-start.2 = ((bf16[8,8,32,256]{3,2,1,0:T(8,128)(2,1)}), bf16[8,8,32,256]{3,2,1,0:T(8,128)(2,1)S(1)}, u32[]{:S(2)}, u32[]{:S(2)}) async-start(bf16[8,8,32,256]{3,2,1,0:T(8,128)(2,1)} %select_up.1), calls=%async_computation.2 | async-start | bytes 2097152 | tf_op jit(solution)/shard_map/all_to_all | solution.py:386
  68.6 10.5 %all-to-all-done.2.slots_ref = bf16[8,8,32,256]{3,2,1,0:T(8,128)(2,1)S(1)} async-done(((bf16[8,8,32,256]{3,2,1,0:T(8,128)(2,1)}), bf16[8,8,32,256]{3,2,1,0:T(8,128)(2,1)S(1)}, u32[]{:S(2)}, u32[]{:S(2)}) %all-to-all-start.2) | async-done | bytes 1048608 | tf_op jit(solution)/shard_map/all_to_all | solution.py:386
  82.3 3.0 %collective-permute-start.18 = (f32[4,32,128]{2,1,0:T(8,128)}, f32[4,32,128]{2,1,0:T(8,128)S(1)}, u32[]{:S(2)}, u32[]{:S(2)}) collective-permute-start(f32[4,32,128]{2,1,0:T(8,128)} %rank_grad_part.1), channel_id=1, source_target_pairs={{0,3},{1,0},{2,1},{3,2},{4,7},{5,4},{6,5},{7,6},{8,11},{9,8},{10,9... | collective-permute-start | bytes 196616 | tf_op jit(solution)/shard_map/ppermute | solution.py:371
  86.3 4.0 %collective-permute-start.4 = (bf16[512,256]{1,0:T(8,128)(2,1)}, bf16[512,256]{1,0:T(8,128)(2,1)S(1)}, u32[]{:S(2)}, u32[]{:S(2)}) collective-permute-start(bf16[512,256]{1,0:T(8,128)(2,1)} %get-tuple-element.45), channel_id=1, source_target_pairs={{0,20},{4,24},{8,28},{12,0},{16,4},{20,8},{24,12},{28,16},{1,21},{... | collective-permute-start | bytes 786440 | tf_op jit(solution)/shard_map/ppermute | solution.py:371
  97.1 8.4 %collective-permute-done.4.refs_5_.refs_13_ = bf16[512,256]{1,0:T(8,128)(2,1)S(1)} collective-permute-done((bf16[512,256]{1,0:T(8,128)(2,1)}, bf16[512,256]{1,0:T(8,128)(2,1)S(1)}, u32[]{:S(2)}, u32[]{:S(2)}) %collective-permute-start.4) | collective-permute-done | bytes 262176 | tf_op jit(solution)/shard_map/ppermute | solution.py:371
  113.1 5.5 %collective-permute-start.21 = (bf16[4,32,128]{2,1,0:T(8,128)(2,1)S(1)}, bf16[4,32,128]{2,1,0:T(8,128)(2,1)S(1)}, u32[]{:S(2)}, u32[]{:S(2)}) collective-permute-start(bf16[4,32,128]{2,1,0:T(8,128)(2,1)S(1)} %multiply_convert_fusion.refs_0_), channel_id=1, source_target_pairs={{0,12},{4,16},{8,20},{12,24},{16,28},{20,0},{24,4},{28,8},{1,13},{... | collective-permute-start | bytes 98312 | tf_op jit(solution)/shard_map/ppermute | solution.py:371
  123.0 6.6 %down_terms.1 = bf16[256,32,256]{2,1,0:T(8,128)(2,1)} custom-call(s32[128]{0:T(128)} %reshape.28.ids_ref, s32[3]{0:T(128)} %pad_add_fusion.me_ref, bf16[4,32,128]{2,1,0:T(8,128)(2,1)} %copy-done.9, bf16[4,32,128]{2,1,0:T(8,128)(2,1)} %copy-done.23, bf16[4,32,128]{2,1,0:T(8,128)(2,1)} %copy-done.22, bf16[4,32,128]{2,1,0:T(8,128)(2,1)} %copy-done.21, ...), custom_call_target="tpu_custom_call" | custom-call | tf_op jit(solution)/shard_map/down_terms/pallas_call | solution.py:170
  129.7 5.9 %rank_part.1 = f32[8,4,32,128]{3,2,1,0:T(8,128)} custom-call(s32[128]{0:T(128)} %reshape.28.ids_ref, s32[3]{0:T(128)} %pad_add_fusion.me_ref, bf16[256,32,256]{2,1,0:T(8,128)(2,1)} %all-gather.3.cloned.1.call-done.table_ref, bf16[512,256]{1,0:T(8,128)(2,1)} %get-tuple-element.50.refs_0_.refs_8_, bf16[512,256]{1,0:T(8,128)(2,1)} %collective-permute-done.refs_1_.refs_9_, ...), custom_call_target="tpu_custom_call" | custom-call | tf_op jit(solution)/shard_map/rank_part/pallas_call | solution.py:211
  135.6 6.2 %all-to-all-start.1 = ((f32[8,4,32,128]{3,2,1,0:T(8,128)}), f32[8,4,32,128]{3,2,1,0:T(8,128)S(1)}, u32[]{:S(2)}, u32[]{:S(2)}) async-start(f32[8,4,32,128]{3,2,1,0:T(8,128)} %rank_part.1), calls=%async_computation.1 | async-start | bytes 1048576 | tf_op jit(solution)/shard_map/all_to_all | solution.py:386
  141.8 5.8 %fusion.9 = f32[512,1024]{1,0:T(8,128)} fusion(bf16[512,2048]{1,0:T(8,128)(2,1)S(1)} %copy-done.3, bf16[2048,1024]{1,0:T(8,128)(2,1)} %refs_4_.1), kind=kOutput, calls=%fused_computation.38 | convolution fusion | flops 2147483648 | bytes 8388608 | tf_op jit(solution)/shard_map/dot_general | solution.py:416
  158.6 5.6 %collective-permute-done.11 = bf16[512,256]{1,0:T(8,128)(2,1)S(1)} collective-permute-done((bf16[512,256]{1,0:T(8,128)(2,1)S(1)}, bf16[512,256]{1,0:T(8,128)(2,1)S(1)}, u32[]{:S(2)}, u32[]{:S(2)}) %collective-permute-start.11) | collective-permute-done | bytes 262176 | tf_op jit(solution)/shard_map/ppermute | solution.py:371
  168.4 2.9 %output_and_up.1 = (bf16[512,256]{1,0:T(8,128)(2,1)}, bf16[8,8,32,256]{3,2,1,0:T(8,128)(2,1)}) custom-call(s32[16]{0:T(128)} %ids_ref.3, bf16[4,32,128]{2,1,0:T(8,128)(2,1)} %add_convert_fusion.rank_ref, bf16[8,8,32,256]{3,2,1,0:T(8,128)(2,1)} %copy-done, bf16[512,256]{1,0:T(8,128)(2,1)} %cot_ref.3, f32[512,256]{1,0:T(8,128)} %convert_add_fusion.base_ref), custom_call_target="tpu_custom_call" | custom-call | tf_op jit(solution)/shard_map/output_and_up/pallas_call | solution.py:277
  171.3 5.0 %all-to-all-start.4 = ((bf16[8,8,32,256]{3,2,1,0:T(8,128)(2,1)}), bf16[8,8,32,256]{3,2,1,0:T(8,128)(2,1)S(1)}, u32[]{:S(2)}, u32[]{:S(2)}) async-start(bf16[8,8,32,256]{3,2,1,0:T(8,128)(2,1)} %get-tuple-element.31), calls=%async_computation.5 | async-start | bytes 2097152 | tf_op jit(solution)/shard_map/all_to_all | solution.py:386
  179.5 6.3 %through_down.1 = (bf16[512,256]{1,0:T(8,128)(2,1)}, bf16[512,256]{1,0:T(8,128)(2,1)}, bf16[512,256]{1,0:T(8,128)(2,1)}, bf16[512,256]{1,0:T(8,128)(2,1)}, bf16[...) custom-call(s32[128]{0:T(128)} %reshape.28.ids_ref, ...), custom_call_target="tpu_custom_call" | custom-call | tf_op jit(solution)/shard_map/through_down/pallas_call | solution.py:250
  196.6 17.4 %collective-permute-start.32 = (bf16[512,256]{1,0:T(8,128)(2,1)}, bf16[512,256]{1,0:T(8,128)(2,1)}, u32[]{:S(2)}, u32[]{:S(2)}) collective-permute-start(bf16[512,256]{1,0:T(8,128)(2,1)} %get-tuple-element.30), channel_id=1, source_target_pairs={{0,4},{4,8},{8,12},{12,16},{16,20},{20,24},{24,28},{28,0},{1,5},{5... | collective-permute-start | bytes 786440 | tf_op jit(solution)/shard_map/ppermute | solution.py:371
  214.0 4.5 %all-to-all-start.3 = ((bf16[8,4,32,256]{3,2,1,0:T(8,128)(2,1)}), bf16[8,4,32,256]{3,2,1,0:T(8,128)(2,1)S(1)}, u32[]{:S(2)}, u32[]{:S(2)}) async-start(bf16[8,4,32,256]{3,2,1,0:T(8,128)(2,1)} %bitcast.55), calls=%async_computation.4 | async-start | bytes 1048576 | tf_op jit(solution)/shard_map/all_to_all | solution.py:386
  218.6 4.2 %gather_up.1 = (f32[4,32,256]{2,1,0:T(8,128)}, bf16[4,32,256]{2,1,0:T(8,128)(2,1)}, bf16[4,32,256]{2,1,0:T(8,128)(2,1)}, bf16[4,32,256]{2,1,0:T(8,128)(2,1)}, bf...) custom-call(s32[128]{0:T(128)} %reshape.28.ids_ref, ...), custom_call_target="tpu_custom_call" | custom-call | tf_op jit(solution)/shard_map/gather_up/pallas_call | solution.py:314
  223.5 2.7 %collective-permute-start.34 = (bf16[4,32,256]{2,1,0:T(8,128)(2,1)}, bf16[4,32,256]{2,1,0:T(8,128)(2,1)S(1)}, u32[]{:S(2)}, u32[]{:S(2)}) collective-permute-start(bf16[4,32,256]{2,1,0:T(8,128)(2,1)} %get-tuple-element.34), channel_id=1, source_target_pairs={{0,64},{32,96},{64,128},{96,160},{128,192},{160,224},{192,0},{224,... | collective-permute-start | bytes 196616 | tf_op jit(solution)/shard_map/ppermute | solution.py:371
  229.5 2.9 %collective-permute-start.37 = (bf16[4,32,256]{2,1,0:T(8,128)(2,1)}, bf16[4,32,256]{2,1,0:T(8,128)(2,1)S(1)}, u32[]{:S(2)}, u32[]{:S(2)}) collective-permute-start(bf16[4,32,256]{2,1,0:T(8,128)(2,1)} %get-tuple-element.37), channel_id=1, source_target_pairs={{0,160},{32,192},{64,224},{96,0},{128,32},{160,64},{192,96},{224,1... | collective-permute-start | bytes 196616 | tf_op jit(solution)/shard_map/ppermute | solution.py:371
  235.3 8.7 %base_gradient.1.base_ref = f32[512,2048]{1,0:T(8,128)} custom-call(s32[3]{0:T(128)} %pad_add_fusion.me_ref, bf16[512,256]{1,0:T(8,128)(2,1)} %cot_ref.3, bf16[512,256]{1,0:T(8,128)(2,1)} %copy-done.12, bf16[512,256]{1,0:T(8,128)(2,1)} %copy-done.11, bf16[512,256]{1,0:T(8,128)(2,1)} %copy-done.10, bf16[2048,1024]{1,0:T(8,128)(2,1)} %refs_4_.1), custom_call_target="tpu_custom_call" | custom-call | tf_op jit(solution)/shard_map/base_gradient/pallas_call | solution.py:338
  244.0 4.5 %input_gradient.1 = bf16[512,2048]{1,0:T(8,128)(2,1)} custom-call(s32[3]{0:T(128)} %pad_add_fusion.me_ref, f32[512,2048]{1,0:T(8,128)} %base_gradient.1.base_ref, bf16[512,256]{1,0:T(8,128)(2,1)} %get-tuple-element.23.refs_0_, bf16[512,256]{1,0:T(8,128)(2,1)} %copy-done.13, bf16[512,256]{1,0:T(8,128)(2,1)} %copy-done.14, bf16[512,256]{1,0:T(8,128)(2,1)} %copy-done.15, ...), custom_call_target="tpu_custom_call" | custom-call | tf_op jit(solution)/shard_map/input_gradient/pallas_call | solution.py:361
  (159 shorter events, 66.9 us)
Async XLA Ops:
  7.2 122.5 %all-gather.3.cloned.1.call-start = ((), (), s32[]{:S(2)}) async-start(), calls=%async_computation.6 | async-start | bytes 4718592 | tf_op jit(solution)/shard_map/all_gather | solution.py:408
  54.9 24.2 %all-to-all-start.2 = ((bf16[8,8,32,256]{3,2,1,0:T(8,128)(2,1)}), bf16[8,8,32,256]{3,2,1,0:T(8,128)(2,1)S(1)}, u32[]{:S(2)}, u32[]{:S(2)}) async-start(bf16[8,8,32,256]{3,2,1,0:T(8,128)(2,1)} %select_up.1), calls=%async_computation.2 | async-start | bytes 2097152 | tf_op jit(solution)/shard_map/all_to_all | solution.py:386
  66.6 147.5 %reduce-scatter.2.cloned.1.call-start = ((), (), s32[]{:S(2)}) async-start(), calls=%async_computation.7 | async-start | bytes 4718592 | tf_op jit(solution)/shard_map/reduce_scatter | solution.py:435
  67.9 18.3 %collective-permute-start.6 = (bf16[512,256]{1,0:T(8,128)(2,1)}, bf16[512,256]{1,0:T(8,128)(2,1)S(1)}, u32[]{:S(2)}, u32[]{:S(2)}) collective-permute-start(bf16[512,256]{1,0:T(8,128)(2,1)} %get-tuple-element.43), channel_id=1, source_target_pairs={{0,28},{4,0},{8,4},{12,8},{16,12},{20,16},{24,20},{28,24},{1,29},{... | collective-permute-start | bytes 786440 | tf_op jit(solution)/shard_map/ppermute | solution.py:371
  68.3 21.9 %collective-permute-start.5 = (bf16[512,256]{1,0:T(8,128)(2,1)}, bf16[512,256]{1,0:T(8,128)(2,1)}, u32[]{:S(2)}, u32[]{:S(2)}) collective-permute-start(bf16[512,256]{1,0:T(8,128)(2,1)} %get-tuple-element.44), channel_id=1, source_target_pairs={{0,24},{4,28},{8,0},{12,4},{16,8},{20,12},{24,16},{28,20},{1,25},{... | collective-permute-start | bytes 786440 | tf_op jit(solution)/shard_map/ppermute | solution.py:371
  86.3 19.2 %collective-permute-start.4 = (bf16[512,256]{1,0:T(8,128)(2,1)}, bf16[512,256]{1,0:T(8,128)(2,1)S(1)}, u32[]{:S(2)}, u32[]{:S(2)}) collective-permute-start(bf16[512,256]{1,0:T(8,128)(2,1)} %get-tuple-element.45), channel_id=1, source_target_pairs={{0,20},{4,24},{8,28},{12,0},{16,4},{20,8},{24,12},{28,16},{1,21},{... | collective-permute-start | bytes 786440 | tf_op jit(solution)/shard_map/ppermute | solution.py:371
  90.2 15.2 %collective-permute-start.3 = (bf16[512,256]{1,0:T(8,128)(2,1)}, bf16[512,256]{1,0:T(8,128)(2,1)S(1)}, u32[]{:S(2)}, u32[]{:S(2)}) collective-permute-start(bf16[512,256]{1,0:T(8,128)(2,1)} %get-tuple-element.46), channel_id=1, source_target_pairs={{0,16},{4,20},{8,24},{12,28},{16,0},{20,4},{24,8},{28,12},{1,17},{... | collective-permute-start | bytes 786440 | tf_op jit(solution)/shard_map/ppermute | solution.py:371
  92.0 17.2 %collective-permute-start.2 = (bf16[512,256]{1,0:T(8,128)(2,1)}, bf16[512,256]{1,0:T(8,128)(2,1)S(1)}, u32[]{:S(2)}, u32[]{:S(2)}) collective-permute-start(bf16[512,256]{1,0:T(8,128)(2,1)} %get-tuple-element.47), channel_id=1, source_target_pairs={{0,12},{4,16},{8,20},{12,24},{16,28},{20,0},{24,4},{28,8},{1,13},{... | collective-permute-start | bytes 786440 | tf_op jit(solution)/shard_map/ppermute | solution.py:371
  92.4 17.4 %collective-permute-start.1 = (bf16[512,256]{1,0:T(8,128)(2,1)}, bf16[512,256]{1,0:T(8,128)(2,1)S(1)}, u32[]{:S(2)}, u32[]{:S(2)}) collective-permute-start(bf16[512,256]{1,0:T(8,128)(2,1)} %get-tuple-element.48), channel_id=1, source_target_pairs={{0,8},{4,12},{8,16},{12,20},{16,24},{20,28},{24,0},{28,4},{1,9},{5... | collective-permute-start | bytes 786440 | tf_op jit(solution)/shard_map/ppermute | solution.py:371
  93.6 19.5 %collective-permute-start = (bf16[512,256]{1,0:T(8,128)(2,1)}, bf16[512,256]{1,0:T(8,128)(2,1)}, u32[]{:S(2)}, u32[]{:S(2)}) collective-permute-start(bf16[512,256]{1,0:T(8,128)(2,1)} %get-tuple-element.49), channel_id=1, source_target_pairs={{0,4},{4,8},{8,12},{12,16},{16,20},{20,24},{24,28},{28,0},{1,5},{5... | collective-permute-start | bytes 786440 | tf_op jit(solution)/shard_map/ppermute | solution.py:371
  135.6 17.2 %all-to-all-start.1 = ((f32[8,4,32,128]{3,2,1,0:T(8,128)}), f32[8,4,32,128]{3,2,1,0:T(8,128)S(1)}, u32[]{:S(2)}, u32[]{:S(2)}) async-start(f32[8,4,32,128]{3,2,1,0:T(8,128)} %rank_part.1), calls=%async_computation.1 | async-start | bytes 1048576 | tf_op jit(solution)/shard_map/all_to_all | solution.py:386
  171.3 42.7 %all-to-all-start.4 = ((bf16[8,8,32,256]{3,2,1,0:T(8,128)(2,1)}), bf16[8,8,32,256]{3,2,1,0:T(8,128)(2,1)S(1)}, u32[]{:S(2)}, u32[]{:S(2)}) async-start(bf16[8,8,32,256]{3,2,1,0:T(8,128)(2,1)} %get-tuple-element.31), calls=%async_computation.5 | async-start | bytes 2097152 | tf_op jit(solution)/shard_map/all_to_all | solution.py:386
  179.3 14.9 %collective-permute-start.13 = (bf16[512,256]{1,0:T(8,128)(2,1)S(1)}, bf16[512,256]{1,0:T(8,128)(2,1)S(1)}, u32[]{:S(2)}, u32[]{:S(2)}) collective-permute-start(bf16[512,256]{1,0:T(8,128)(2,1)S(1)} %copy-done.2), channel_id=1, source_target_pairs={{0,1},{1,2},{2,3},{3,0},{4,5},{5,6},{6,7},{7,4},{8,9},{9,10},{10,1... | collective-permute-start | bytes 786440 | tf_op jit(solution)/shard_map/ppermute | solution.py:371
  189.6 33.2 %collective-permute-start.28 = (bf16[512,256]{1,0:T(8,128)(2,1)}, bf16[512,256]{1,0:T(8,128)(2,1)S(1)}, u32[]{:S(2)}, u32[]{:S(2)}) collective-permute-start(bf16[512,256]{1,0:T(8,128)(2,1)} %get-tuple-element.26), channel_id=1, source_target_pairs={{0,20},{4,24},{8,28},{12,0},{16,4},{20,8},{24,12},{28,16},{1,21},{... | collective-permute-start | bytes 786440 | tf_op jit(solution)/shard_map/ppermute | solution.py:371
  191.2 32.4 %collective-permute-start.29 = (bf16[512,256]{1,0:T(8,128)(2,1)}, bf16[512,256]{1,0:T(8,128)(2,1)S(1)}, u32[]{:S(2)}, u32[]{:S(2)}) collective-permute-start(bf16[512,256]{1,0:T(8,128)(2,1)} %get-tuple-element.27), channel_id=1, source_target_pairs={{0,16},{4,20},{8,24},{12,28},{16,0},{20,4},{24,8},{28,12},{1,17},{... | collective-permute-start | bytes 786440 | tf_op jit(solution)/shard_map/ppermute | solution.py:371
  194.2 32.0 %collective-permute-start.30 = (bf16[512,256]{1,0:T(8,128)(2,1)}, bf16[512,256]{1,0:T(8,128)(2,1)}, u32[]{:S(2)}, u32[]{:S(2)}) collective-permute-start(bf16[512,256]{1,0:T(8,128)(2,1)} %get-tuple-element.28), channel_id=1, source_target_pairs={{0,12},{4,16},{8,20},{12,24},{16,28},{20,0},{24,4},{28,8},{1,13},{... | collective-permute-start | bytes 786440 | tf_op jit(solution)/shard_map/ppermute | solution.py:371
  195.8 31.9 %collective-permute-start.31 = (bf16[512,256]{1,0:T(8,128)(2,1)}, bf16[512,256]{1,0:T(8,128)(2,1)}, u32[]{:S(2)}, u32[]{:S(2)}) collective-permute-start(bf16[512,256]{1,0:T(8,128)(2,1)} %get-tuple-element.29), channel_id=1, source_target_pairs={{0,8},{4,12},{8,16},{12,20},{16,24},{20,28},{24,0},{28,4},{1,9},{5... | collective-permute-start | bytes 786440 | tf_op jit(solution)/shard_map/ppermute | solution.py:371
  196.6 32.9 %collective-permute-start.32 = (bf16[512,256]{1,0:T(8,128)(2,1)}, bf16[512,256]{1,0:T(8,128)(2,1)}, u32[]{:S(2)}, u32[]{:S(2)}) collective-permute-start(bf16[512,256]{1,0:T(8,128)(2,1)} %get-tuple-element.30), channel_id=1, source_target_pairs={{0,4},{4,8},{8,12},{12,16},{16,20},{20,24},{24,28},{28,0},{1,5},{5... | collective-permute-start | bytes 786440 | tf_op jit(solution)/shard_map/ppermute | solution.py:371
  214.0 35.3 %all-to-all-start.3 = ((bf16[8,4,32,256]{3,2,1,0:T(8,128)(2,1)}), bf16[8,4,32,256]{3,2,1,0:T(8,128)(2,1)S(1)}, u32[]{:S(2)}, u32[]{:S(2)}) async-start(bf16[8,4,32,256]{3,2,1,0:T(8,128)(2,1)} %bitcast.55), calls=%async_computation.4 | async-start | bytes 1048576 | tf_op jit(solution)/shard_map/all_to_all | solution.py:386
  226.2 22.3 %collective-permute-start.35 = (bf16[4,32,256]{2,1,0:T(8,128)(2,1)}, bf16[4,32,256]{2,1,0:T(8,128)(2,1)S(1)}, u32[]{:S(2)}, u32[]{:S(2)}) collective-permute-start(bf16[4,32,256]{2,1,0:T(8,128)(2,1)} %get-tuple-element.35), channel_id=1, source_target_pairs={{0,96},{32,128},{64,160},{96,192},{128,224},{160,0},{192,32},{224,... | collective-permute-start | bytes 196616 | tf_op jit(solution)/shard_map/ppermute | solution.py:371
  227.7 20.9 %collective-permute-start.36 = (bf16[4,32,256]{2,1,0:T(8,128)(2,1)}, bf16[4,32,256]{2,1,0:T(8,128)(2,1)S(1)}, u32[]{:S(2)}, u32[]{:S(2)}) collective-permute-start(bf16[4,32,256]{2,1,0:T(8,128)(2,1)} %get-tuple-element.36), channel_id=1, source_target_pairs={{0,128},{32,160},{64,192},{96,224},{128,0},{160,32},{192,64},{224,... | collective-permute-start | bytes 196616 | tf_op jit(solution)/shard_map/ppermute | solution.py:371
  229.5 19.0 %collective-permute-start.37 = (bf16[4,32,256]{2,1,0:T(8,128)(2,1)}, bf16[4,32,256]{2,1,0:T(8,128)(2,1)S(1)}, u32[]{:S(2)}, u32[]{:S(2)}) collective-permute-start(bf16[4,32,256]{2,1,0:T(8,128)(2,1)} %get-tuple-element.37), channel_id=1, source_target_pairs={{0,160},{32,192},{64,224},{96,0},{128,32},{160,64},{192,96},{224,1... | collective-permute-start | bytes 196616 | tf_op jit(solution)/shard_map/ppermute | solution.py:371
  232.4 16.1 %collective-permute-start.38 = (bf16[4,32,256]{2,1,0:T(8,128)(2,1)}, bf16[4,32,256]{2,1,0:T(8,128)(2,1)S(1)}, u32[]{:S(2)}, u32[]{:S(2)}) collective-permute-start(bf16[4,32,256]{2,1,0:T(8,128)(2,1)} %get-tuple-element.38), channel_id=1, source_target_pairs={{0,192},{32,224},{64,0},{96,32},{128,64},{160,96},{192,128},{224,1... | collective-permute-start | bytes 196616 | tf_op jit(solution)/shard_map/ppermute | solution.py:371
  232.9 15.7 %collective-permute-start.39 = (bf16[4,32,256]{2,1,0:T(8,128)(2,1)}, bf16[4,32,256]{2,1,0:T(8,128)(2,1)S(1)}, u32[]{:S(2)}, u32[]{:S(2)}) collective-permute-start(bf16[4,32,256]{2,1,0:T(8,128)(2,1)} %get-tuple-element.39), channel_id=1, source_target_pairs={{0,224},{32,0},{64,32},{96,64},{128,96},{160,128},{192,160},{224,1... | collective-permute-start | bytes 196616 | tf_op jit(solution)/shard_map/ppermute | solution.py:371
  (48 other events, 699.7 us)
Sparse Core Ops, SparseCore 0:
  23.1 58.0 all-gather.2
  129.8 52.4 reduce-scatter.1
where the time goes:
time: 262 us; the launch traced here: 257 us
  starting transfers between devices  98.9 us (38%)
  Pallas kernels  45.5 us (17%)
  blocking collectives  39.6 us (15%)
  waiting for transfers between devices  38.7 us (15%)
  between operations  14.4 us (5%)
  local copies, waits for them, and re-layouts  7.65 us (3%)
  other arithmetic  6.68 us (3%)
  matrix products  5.84 us (2%)
    ppermute x40, starting transfers between devices, shift(): return lax.ppermute(x, axis, [(i, (i + k) % size) for i in range(size)])  71.5 us
    ppermute x40, waiting for transfers between devices, shift(): return lax.ppermute(x, axis, [(i, (i + k) % size) for i in range(size)])  28.2 us
    all_to_all x4, starting transfers between devices, exchange(): return lax.all_to_all(x, axis, split_axis=0, concat_axis=0, tiled=True)  27.4 us
    all_gather x1, blocking collectives, step(): up_all = lax.all_gather(adapter_up, 'z', axis=0)  26.6 us
    all_to_all x1, blocking collectives, exchange(): return lax.all_to_all(x, axis, split_axis=0, concat_axis=0, tiled=True)  13 us
    all_to_all x4, waiting for transfers between devices, exchange(): return lax.all_to_all(x, axis, split_axis=0, concat_axis=0, tiled=True)  10.5 us
    pallas_call x1, Pallas kernels, base_gradient(): pl.pallas_call(kernel, grid=(features // tile,), in_specs=[SMEM()] + [pl....  8.66 us
    pallas_call x1, Pallas kernels, down_terms(): pl.pallas_call(kernel, in_specs=[SMEM(), SMEM()] + [HBM()] * (2 * plane),...  6.64 us
  transfers between devices with their start and end apart: 46, of which 12 were waited for; matrix products, arithmetic and copies ran while one was open for 6% of the time, Pallas kernels for 18%

commit v1 on v0

--- a/solution.py
+++ b/solution.py
@@ -81,11 +81,12 @@
             @pl.when(lax.rem(owner, plane) == my_g)
             def _():
                 z = lax.div(owner, plane)
-                out_ref[lax.div(b, blocks), z] = all_ref[z, lax.rem(number, owned)]
-
-            return carry
-
-        lax.fori_loop(0, plane * blocks, step, 0, unroll=4)
+                dest = back(my_g, lax.div(b, blocks), plane)
+                out_ref[dest, z] = all_ref[z, lax.rem(number, owned)]
+
+            return carry
+
+        lax.fori_loop(0, plane * blocks, step, 0, unroll=2)
 
     return pl.pallas_call(
         kernel,
@@ -149,13 +150,12 @@
         def step(k, carry):
             loaded(rgs, rg_stack, rg_sems, k)
             loaded(toks, tok_stack, tok_sems, k)
-            src = back(me_ref[1], k, plane)
             for q in range(quads):
                 wide = spread(rg_stack[k, q], mask)
                 rows = tok_stack[k, q * span : (q + 1) * span, :]
                 got = dot_tn(wide, rows) * (1.0 / length)
                 for i in range(QUAD):
-                    a = ids_ref[src * blocks + q * QUAD + i]
+                    a = ids_ref[k * blocks + q * QUAD + i]
                     acc[a] = acc[a] + got[i * rank : (i + 1) * rank]
             return carry
 
@@ -201,7 +201,7 @@
             dest = back(me_ref[1], k, plane)
             loaded(toks, stack, sems, k)
             for q in range(quads):
-                down = table_rows(ids_ref, table_ref, dest * blocks + q * QUAD)
+                down = table_rows(ids_ref, table_ref, k * blocks + q * QUAD)
                 got = dot_nt(stack[k, q * span : (q + 1) * span, :], down)
                 out_ref[dest, q] = fold(got, mask, length)
             return carry
@@ -234,9 +234,8 @@
 
         def step(k, carry):
             loaded(rgs, rg_stack, rg_sems, k)
-            src = back(me_ref[1], k, plane)
             for q in range(quads):
-                down = table_rows(ids_ref, table_ref, src * blocks + q * QUAD)
+                down = table_rows(ids_ref, table_ref, k * blocks + q * QUAD)
                 got = dot_nn(spread(rg_stack[k, q], mask), down)
                 stack[k, q * span : (q + 1) * span, :] = got.astype(bf)
             return carry
@@ -290,9 +289,8 @@
     plane, planes, rank, cols = got.shape
     blocks = ids_all.shape[0] // plane
 
-    def kernel(ids_ref, me_ref, got_ref, *refs):
-        outs, acc = refs[:planes], refs[planes]
-        my_z, my_g = me_ref[0], me_ref[1]
+    def kernel(ids_ref, me_ref, got_ref, out_ref, acc):
+        my_g = me_ref[1]
         acc[...] = jnp.zeros(acc.shape, f32)
 
         def step(b, carry):
@@ -302,69 +300,123 @@
             @pl.when(lax.rem(owner, plane) == my_g)
             def _():
                 z, local = lax.div(owner, plane), lax.rem(number, owned)
-                acc[z, local] = acc[z, local] + got_ref[lax.div(b, blocks), z].astype(f32)
-
-            return carry
-
-        lax.fori_loop(0, plane * blocks, step, 0, unroll=4)
-        for k in range(planes):
-            outs[k][...] = acc[lax.rem(my_z + k, planes)].astype(outs[k].dtype)
-
-    chunk = (owned, rank, cols)
+                acc[z, local] = acc[z, local] + got_ref[back(my_g, lax.div(b, blocks), plane), z].astype(f32)
+
+            return carry
+
+        lax.fori_loop(0, plane * blocks, step, 0, unroll=2)
+        out_ref[...] = acc[...].astype(bf)
+
+    shape = (planes, owned, rank, cols)
     return pl.pallas_call(
         kernel,
         in_specs=[SMEM(), SMEM(), VMEM()],
-        out_specs=tuple([VMEM()] * planes),
-        out_shape=tuple(jax.ShapeDtypeStruct(chunk, bf if k else f32) for k in range(planes)),
-        scratch_shapes=[pltpu.VMEM((planes,) + chunk, f32)],
+        out_specs=VMEM(),
+        out_shape=jax.ShapeDtypeStruct(shape, bf),
+        scratch_shapes=[pltpu.VMEM(shape, f32)],
         name="gather_up",
     )(ids_all, me, got)
 
 
-def base_gradient(me, cots, weight):
-    parts = len(cots)
+def input_gradient(me, cots, weight, through):
+    parts, plane = len(cots), len(through)
     tokens, cols = cots[0].shape
-    features = weight.shape[0]
-    tile = 256
+    narrow = through[0].shape[1]
+
+    def ahead(i, me_ref):
+        return lax.rem(me_ref[1] + i, plane)
 
     def kernel(me_ref, *refs):
-        w_ref, out_ref = refs[parts], refs[parts + 1]
-        total = jnp.zeros((tokens, tile), f32)
+        cot_refs, w_ref, thr_refs = refs[:parts], refs[parts], refs[parts + 1 : parts + 1 + plane]
+        out_ref, stack, sems = refs[parts + 1 + plane :]
+        i = pl.program_id(0)
+
+        @pl.when(i == 0)
+        def _():
+            load(thr_refs, stack, sems)
+
+        loaded(thr_refs, stack, sems, i)
+        total = stack[i].astype(f32)
         for k in range(parts):
             first = pl.multiple_of(back(me_ref[2], k, parts) * cols, cols)
-            total = total + dot_nt(refs[k][...], w_ref[:, pl.ds(first, cols)])
-        out_ref[...] = total
-
-    return pl.pallas_call(
-        kernel,
-        grid=(features // tile,),
-        in_specs=[SMEM()]
-        + [pl.BlockSpec((tokens, cols), lambda s: (0, 0))] * parts
-        + [pl.BlockSpec((tile, parts * cols), lambda s: (s, 0))],
-        out_specs=pl.BlockSpec((tokens, tile), lambda s: (0, s)),
-        out_shape=jax.ShapeDtypeStruct((tokens, features), f32),
-        name="base_gradient",
-    )(me, *cots, weight)
-
-
-def input_gradient(me, base, through):
-    plane = len(through)
-    tokens, narrow = through[0].shape
-
-    def kernel(me_ref, base_ref, *refs):
+            total = total + dot_nt(cot_refs[k][...], w_ref[:, pl.ds(first, cols)])
+        out_ref[...] = total.astype(bf)
+
+    return pl.pallas_call(
+        kernel,
+        grid_spec=pltpu.PrefetchScalarGridSpec(
+            num_scalar_prefetch=1,
+            grid=(plane,),
+            in_specs=[pl.BlockSpec((tokens, cols), lambda i, me_ref: (0, 0))] * parts
+            + [pl.BlockSpec((narrow, parts * cols), lambda i, me_ref: (ahead(i, me_ref), 0))]
+            + [HBM()] * plane,
+            out_specs=pl.BlockSpec((tokens, narrow), lambda i, me_ref: (0, ahead(i, me_ref))),
+            scratch_shapes=stacked(plane, through[0]),
+        ),
+        out_shape=jax.ShapeDtypeStruct((tokens, plane * narrow), bf),
+        name="input_gradient",
+    )(me, *cots, weight, *through)
+
+
+def pack_down(me, down, tile, plane):
+    rows, width = down.shape
+    narrow = width // plane
+    piece = jax.ShapeDtypeStruct((rows + tile.shape[0], narrow), bf)
+
+    def kernel(me_ref, down_ref, tile_ref, *outs):
+        for k in range(plane):
+            first = pl.multiple_of(lax.rem(me_ref[1] + k, plane) * narrow, narrow)
+            outs[k][:rows, :] = down_ref[:, pl.ds(first, narrow)]
+            outs[k][rows:, :] = tile_ref[...]
+
+    return pl.pallas_call(
+        kernel,
+        in_specs=[SMEM(), VMEM(), VMEM()],
+        out_specs=tuple([VMEM()] * plane),
+        out_shape=tuple([piece] * plane),
+        name="pack_down",
+    )(me, down, tile)
+
+
+def unpack_down(pieces, rows):
+    plane = len(pieces)
+    narrow = pieces[0].shape[1]
+
+    def kernel(*refs):
+        down_ref, ids_ref = refs[plane:]
+        for k in range(plane):
+            down_ref[k] = refs[k][:rows, :]
+            ids_ref[k : k + 1, :] = refs[k][rows : rows + 1, :128].astype(f32).astype(jnp.int32)
+
+    return pl.pallas_call(
+        kernel,
+        in_specs=[VMEM()] * plane,
+        out_specs=(VMEM(), VMEM()),
+        out_shape=(
+            jax.ShapeDtypeStruct((plane, rows, narrow), bf),
+            jax.ShapeDtypeStruct((plane, 128), jnp.int32),
+        ),
+        name="unpack_down",
+    )(*pieces)
+
+
+def down_gradient(me, pieces):
+    plane = len(pieces)
+    owned, rank, narrow = pieces[0].shape
+
+    def kernel(me_ref, *refs):
         out_ref = refs[plane]
         for k in range(plane):
-            first = pl.multiple_of(lax.rem(me_ref[1] + k, plane) * narrow, narrow)
-            cols = pl.ds(first, narrow)
-            out_ref[:, cols] = (base_ref[:, cols] + refs[k][...].astype(f32)).astype(bf)
-
-    return pl.pallas_call(
-        kernel,
-        in_specs=[SMEM()] + [VMEM()] * (plane + 1),
+            first = pl.multiple_of(back(me_ref[1], k, plane) * narrow, narrow)
+            out_ref[:, :, pl.ds(first, narrow)] = refs[k][...].astype(f32)
+
+    return pl.pallas_call(
+        kernel,
+        in_specs=[SMEM()] + [VMEM()] * plane,
         out_specs=VMEM(),
-        out_shape=jax.ShapeDtypeStruct((tokens, plane * narrow), bf),
-        name="input_gradient",
-    )(me, base, *through)
+        out_shape=jax.ShapeDtypeStruct((owned, rank, plane * narrow), f32),
+        name="down_gradient",
+    )(me, *pieces)
 
 
 def shift(x, axis, size, k):
@@ -385,9 +437,6 @@
     def exchange(x, axis="g"):
         return lax.all_to_all(x, axis, split_axis=0, concat_axis=0, tiled=True)
 
-    def sliced(x):
-        return x.reshape(owned, rank, plane, narrow).transpose(2, 0, 1, 3)
-
     def mp_sum(x):
         total = x
         for k in range(1, parts):
@@ -395,24 +444,23 @@
         return total
 
     ids = block_adapter
-    up_all = lax.all_gather(adapter_up, "z", axis=0)
-    tile = jnp.pad(ids.astype(bf)[None, None], ((0, 0), (0, 15), (0, narrow - blocks)))
-    sent = jnp.concatenate(
-        [sliced(adapter_down).reshape(plane, owned * rank, narrow)]
-        + [jnp.broadcast_to(tile, (plane, 16, narrow))],
-        axis=1,
-    )
-    got = exchange(sent)
-    ids_all = got[:, owned * rank, :blocks].astype(jnp.int32).reshape(-1)
-    down_n = got[:, : owned * rank].reshape(plane * owned, rank, narrow)
-    table = lax.all_gather(down_n, "z", axis=0, tiled=True)
+    up_all = exchange(jnp.broadcast_to(adapter_up[None], (planes,) + adapter_up.shape), "z")
+    rows = owned * rank
+    tile = jnp.pad(ids.astype(bf)[None], ((0, 15), (0, narrow - blocks)))
+    packed = pack_down(me, adapter_down.reshape(rows, width_local), tile, plane)
+    got = [packed[0]] + [shift(packed[k], "g", plane, k) for k in range(1, plane)]
+    down_n, ids_rows = unpack_down(got, rows)
+    table = lax.all_gather(down_n.reshape(-1, rank, narrow), "z", axis=0, tiled=True)
+    ids_all = ids_rows[:, :blocks].reshape(-1)
+    owner = ids_all // owned
+    steps = lax.rem(my_g - owner % plane + plane, plane)
+    ids_row = (owner // plane * plane + steps) * owned + ids_all % owned
     tok_n = []
     for k in range(plane):
         first = lax.rem(my_g + k, plane) * narrow
         part = lax.dynamic_slice_in_dim(tokens, first, narrow, axis=1)
         tok_n.append(shift(part, "g", plane, k) if k else part)
     cots = [cotangent] + [shift(cotangent, "mp", parts, k) for k in range(1, parts)]
-    base_grad = base_gradient(me, cots, base_weight)
     base_part = jnp.dot(tokens, base_weight, preferred_element_type=f32)
 
     def columns(k):
@@ -429,26 +477,29 @@
     rg = (adapter_scale * mp_sum(rg_part)).astype(bf)
     rg_all = [rg] + [shift(rg, "g", plane, k) for k in range(1, plane)]
 
-    part = rank_part(ids_all, me, table, tok_n)
+    part = rank_part(ids_row, me, table, tok_n)
     rank_parts = exchange(part)
     grad_table = down_terms(ids_all, me, rg_all, tok_n, adapters, rank)
     grad_n = lax.psum_scatter(grad_table, "z", scatter_dimension=0, tiled=True)
-    grad_got = exchange(grad_n.reshape(plane, owned, rank, narrow))
-    down_grad = jnp.concatenate([grad_got[i] for i in range(plane)], axis=-1).astype(f32)
+    chunks = grad_n.reshape(plane, owned, rank, narrow)
+    grad_got = []
+    for k in range(plane):
+        part = lax.dynamic_index_in_dim(chunks, lax.rem(my_g + k, plane), 0, keepdims=False)
+        grad_got.append(shift(part, "g", plane, k) if k else part)
+    down_grad = down_gradient(me, grad_got)
 
     ranks = mp_sum(jnp.sum(rank_parts, axis=0)).astype(bf)
 
-    through_n = through_down(ids_all, me, table, rg_all)
+    through_n = through_down(ids_row, me, table, rg_all)
     through = [through_n[0]]
     through += [shift(through_n[k], "g", plane, plane - k) for k in range(1, plane)]
-    input_grad = input_gradient(me, base_grad, through)
+    input_grad = input_gradient(me, cots, base_weight, through)
 
     output, up_send = output_and_up(ids, ranks, slots, cotangent, frozen, owned)
     up_got = exchange(up_send)
     up_chunks = gather_up(ids_all, me, up_got, owned)
-    up_grad = up_chunks[0]
-    for k in range(1, planes):
-        up_grad = up_grad + shift(up_chunks[k], "z", planes, k).astype(f32)
+    up_got = exchange(up_chunks, "z")
+    up_grad = jnp.sum(up_got.astype(f32), axis=0)
     return (output, input_grad, down_grad, up_grad)
 
 

time: 262 us -> 277 us (1.057)
  waiting for transfers between devices: 38.7 us -> 62.9 us
  blocking collectives: 39.6 us -> 18.6 us
  starting transfers between devices: 98.9 us -> 105 us
  local copies, waits for them, and re-layouts: 7.65 us -> 12.5 us
  Pallas kernels: 45.5 us -> 48.5 us
    all_gather x1 -> x0, blocking collectives: 26.6 us -> none  [step(): up_all = lax.all_gather(adapter_up, 'z', axis=0)]
    all_to_all x4, waiting for transfers between devices: 10.5 us -> 27.2 us  [exchange(): return lax.all_to_all(x, axis, split_axis=0, concat_axis=0, tiled=True)]
    ppermute x40 -> x47, waiting for transfers between devices: 28.2 us -> 35.6 us  [shift(): return lax.ppermute(x, axis, [(i, (i + k) % size) for i in range(size)])]
    all_to_all x1, blocking collectives: 13 us -> 18.6 us  [exchange(): return lax.all_to_all(x, axis, split_axis=0, concat_axis=0, tiled=True)]
    ppermute x40 -> x47, starting transfers between devices: 71.5 us -> 75.3 us  [shift(): return lax.ppermute(x, axis, [(i, (i + k) % size) for i in range(size)])]
    pallas_call x3 -> x5, Pallas kernels: 17.4 us -> 20.3 us  [the longest x1 9.88 us: input_gradient(): pl.pallas_call(kernel, grid_spec=pltpu.PrefetchScalarGridSpec(num_scalar_...]
  transfers between devices with their start and end apart: 46 -> 53, of which waited for: 12 -> 22; matrix products, arithmetic and copies ran while one was open for 6% -> 6% of each run, Pallas kernels for 18% -> 16%
where the time goes in v1:
time: 277 us; the launch traced here: 273 us
  starting transfers between devices  105 us (38%)
  waiting for transfers between devices  62.9 us (23%)
  Pallas kernels  48.5 us (18%)
  blocking collectives  18.6 us (7%)
  between operations  14.4 us (5%)
  local copies, waits for them, and re-layouts  12.5 us (5%)
  other arithmetic  6.01 us (2%)
  matrix products  5.89 us (2%)
    ppermute x47, starting transfers between devices, shift(): return lax.ppermute(x, axis, [(i, (i + k) % size) for i in range(size)])  75.3 us
    ppermute x47, waiting for transfers between devices, shift(): return lax.ppermute(x, axis, [(i, (i + k) % size) for i in range(size)])  35.6 us
    all_to_all x4, starting transfers between devices, exchange(): return lax.all_to_all(x, axis, split_axis=0, concat_axis=0, tiled=True)  29.4 us
    all_to_all x4, waiting for transfers between devices, exchange(): return lax.all_to_all(x, axis, split_axis=0, concat_axis=0, tiled=True)  27.2 us
    all_to_all x1, blocking collectives, exchange(): return lax.all_to_all(x, axis, split_axis=0, concat_axis=0, tiled=True)  18.6 us
    pallas_call x1, Pallas kernels, input_gradient(): pl.pallas_call(kernel, grid_spec=pltpu.PrefetchScalarGridSpec(num_scalar_...  9.88 us
    pallas_call x1, Pallas kernels, down_terms(): pl.pallas_call(kernel, in_specs=[SMEM(), SMEM()] + [HBM()] * (2 * plane),...  6.65 us
    pallas_call x1, Pallas kernels, through_down(): pl.pallas_call(kernel, in_specs=[SMEM(), SMEM(), VMEM()] + [HBM()] * plan...  6.17 us
  transfers between devices with their start and end apart: 53, of which 22 were waited for; matrix products, arithmetic and copies ran while one was open for 6% of the time, Pallas kernels for 16%

profile of v1, /device:TPU:37, one launch (start us, length us, event | category | flops | bytes accessed | tf_op | source)
XLA Modules:
  0.0 273.4 jit_solution(14540936688842306337)
XLA Ops:
  27.0 8.0 %all-to-all-start.1 = ((bf16[8,4,32,256]{3,2,1,0:T(8,128)(2,1)}), bf16[8,4,32,256]{3,2,1,0:T(8,128)(2,1)S(1)}, u32[]{:S(2)}, u32[]{:S(2)}) async-start(bf16[8,4,32,256]{3,2,1,0:T(8,128)(2,1)} %broadcast_in_dim.10), calls=%async_computation.1 | async-start | bytes 1048576 | tf_op jit(solution)/shard_map/all_to_all | solution.py:438
  35.7 17.1 %all-to-all-done.1.all_ref = bf16[8,4,32,256]{3,2,1,0:T(8,128)(2,1)S(1)} async-done(((bf16[8,4,32,256]{3,2,1,0:T(8,128)(2,1)}), bf16[8,4,32,256]{3,2,1,0:T(8,128)(2,1)S(1)}, u32[]{:S(2)}, u32[]{:S(2)}) %all-to-all-start.1) | async-done | bytes 524320 | tf_op jit(solution)/shard_map/all_to_all | solution.py:438
  53.6 4.3 %select_up.1 = bf16[8,8,32,256]{3,2,1,0:T(8,128)(2,1)} custom-call(s32[128]{0:T(128)} %reshape.22.ids_ref, s32[3]{0:T(128)} %pad_add_fusion.me_ref, bf16[8,4,32,256]{3,2,1,0:T(8,128)(2,1)} %copy-done.3), custom_call_target="tpu_custom_call" | custom-call | tf_op jit(solution)/shard_map/select_up/pallas_call | solution.py:91
  57.9 9.0 %all-to-all-start.2 = ((bf16[8,8,32,256]{3,2,1,0:T(8,128)(2,1)}), bf16[8,8,32,256]{3,2,1,0:T(8,128)(2,1)S(1)}, u32[]{:S(2)}, u32[]{:S(2)}) async-start(bf16[8,8,32,256]{3,2,1,0:T(8,128)(2,1)} %select_up.1), calls=%async_computation.2 | async-start | bytes 2097152 | tf_op jit(solution)/shard_map/all_to_all | solution.py:438
  69.4 10.1 %all-to-all-done.2.slots_ref = bf16[8,8,32,256]{3,2,1,0:T(8,128)(2,1)S(1)} async-done(((bf16[8,8,32,256]{3,2,1,0:T(8,128)(2,1)}), bf16[8,8,32,256]{3,2,1,0:T(8,128)(2,1)S(1)}, u32[]{:S(2)}, u32[]{:S(2)}) %all-to-all-start.2) | async-done | bytes 1048608 | tf_op jit(solution)/shard_map/all_to_all | solution.py:438
  82.7 2.9 %collective-permute-start.25 = (f32[4,32,128]{2,1,0:T(8,128)}, f32[4,32,128]{2,1,0:T(8,128)S(1)}, u32[]{:S(2)}, u32[]{:S(2)}) collective-permute-start(f32[4,32,128]{2,1,0:T(8,128)} %rank_grad_part.1), channel_id=1, source_target_pairs={{0,3},{1,0},{2,1},{3,2},{4,7},{5,4},{6,5},{7,6},{8,11},{9,8},{10,9... | collective-permute-start | bytes 196616 | tf_op jit(solution)/shard_map/ppermute | solution.py:423
  86.6 4.7 %collective-permute-start.9 = (bf16[512,256]{1,0:T(8,128)(2,1)}, bf16[512,256]{1,0:T(8,128)(2,1)S(1)}, u32[]{:S(2)}, u32[]{:S(2)}) collective-permute-start(bf16[512,256]{1,0:T(8,128)(2,1)} %get-tuple-element.51), channel_id=1, source_target_pairs={{0,12},{4,16},{8,20},{12,24},{16,28},{20,0},{24,4},{28,8},{1,13},{... | collective-permute-start | bytes 786440 | tf_op jit(solution)/shard_map/ppermute | solution.py:423
  97.5 8.6 %collective-permute-start.26 = (bf16[4,32,128]{2,1,0:T(8,128)(2,1)S(1)}, bf16[4,32,128]{2,1,0:T(8,128)(2,1)S(1)}, u32[]{:S(2)}, u32[]{:S(2)}) collective-permute-start(bf16[4,32,128]{2,1,0:T(8,128)(2,1)S(1)} %multiply_convert_fusion.refs_0_), channel_id=1, source_target_pairs={{0,4},{4,8},{8,12},{12,16},{16,20},{20,24},{24,28},{28,0},{1,5},{5... | collective-permute-start | bytes 98312 | tf_op jit(solution)/shard_map/ppermute | solution.py:423
  109.8 4.8 %collective-permute-done.12.refs_6_.refs_14_ = bf16[512,256]{1,0:T(8,128)(2,1)S(1)} collective-permute-done((bf16[512,256]{1,0:T(8,128)(2,1)}, bf16[512,256]{1,0:T(8,128)(2,1)S(1)}, u32[]{:S(2)}, u32[]{:S(2)}) %collective-permute-start.12) | collective-permute-done | bytes 262176 | tf_op jit(solution)/shard_map/ppermute | solution.py:423
  122.9 6.7 %down_terms.1 = bf16[256,32,256]{2,1,0:T(8,128)(2,1)} custom-call(s32[128]{0:T(128)} %reshape.22.ids_ref, s32[3]{0:T(128)} %pad_add_fusion.me_ref, bf16[4,32,128]{2,1,0:T(8,128)(2,1)} %copy-done.9, bf16[4,32,128]{2,1,0:T(8,128)(2,1)} %copy-done.20, bf16[4,32,128]{2,1,0:T(8,128)(2,1)} %copy-done.21, bf16[4,32,128]{2,1,0:T(8,128)(2,1)} %copy-done.22, ...), custom_call_target="tpu_custom_call" | custom-call | tf_op jit(solution)/shard_map/down_terms/pallas_call | solution.py:170
  130.8 5.9 %rank_part.1 = f32[8,4,32,128]{3,2,1,0:T(8,128)} custom-call(s32[128]{0:T(128)} %fusion.ids_ref, s32[3]{0:T(128)} %pad_add_fusion.me_ref, bf16[256,32,256]{2,1,0:T(8,128)(2,1)} %all-gather.2.cloned.1.call-done.table_ref, bf16[512,256]{1,0:T(8,128)(2,1)} %get-tuple-element.54.refs_0_.refs_8_, bf16[512,256]{1,0:T(8,128)(2,1)} %copy-done.4, ...), custom_call_target="tpu_custom_call" | custom-call | tf_op jit(solution)/shard_map/rank_part/pallas_call | solution.py:211
  136.7 6.8 %all-to-all-start = ((f32[8,4,32,128]{3,2,1,0:T(8,128)}), f32[8,4,32,128]{3,2,1,0:T(8,128)S(1)}, u32[]{:S(2)}, u32[]{:S(2)}) async-start(f32[8,4,32,128]{3,2,1,0:T(8,128)} %rank_part.1), calls=%async_computation | async-start | bytes 1048576 | tf_op jit(solution)/shard_map/all_to_all | solution.py:438
  143.5 5.9 %fusion.5 = f32[512,1024]{1,0:T(8,128)} fusion(bf16[512,2048]{1,0:T(8,128)(2,1)S(1)} %copy-done.2, bf16[2048,1024]{1,0:T(8,128)(2,1)} %refs_4_.1), kind=kOutput, calls=%fused_computation.42 | convolution fusion | flops 2147483648 | bytes 8388608 | tf_op jit(solution)/shard_map/dot_general | solution.py:464
  161.6 7.3 %collective-permute-done.17 = bf16[512,256]{1,0:T(8,128)(2,1)S(1)} collective-permute-done((bf16[512,256]{1,0:T(8,128)(2,1)S(1)}, bf16[512,256]{1,0:T(8,128)(2,1)S(1)}, u32[]{:S(2)}, u32[]{:S(2)}) %collective-permute-start.17) | collective-permute-done | bytes 262176 | tf_op jit(solution)/shard_map/ppermute | solution.py:423
  171.5 2.9 %output_and_up.1 = (bf16[512,256]{1,0:T(8,128)(2,1)}, bf16[8,8,32,256]{3,2,1,0:T(8,128)(2,1)}) custom-call(s32[16]{0:T(128)} %ids_ref.3, bf16[4,32,128]{2,1,0:T(8,128)(2,1)} %add_convert_fusion.rank_ref, bf16[8,8,32,256]{3,2,1,0:T(8,128)(2,1)} %copy-done, bf16[512,256]{1,0:T(8,128)(2,1)} %refs_0_.1, f32[512,256]{1,0:T(8,128)} %convert_add_fusion.base_ref), custom_call_target="tpu_custom_call" | custom-call | tf_op jit(solution)/shard_map/output_and_up/pallas_call | solution.py:276
  174.4 18.6 %all_to_all.25.got_ref = bf16[8,8,32,256]{3,2,1,0:T(8,128)(2,1)} all-to-all(bf16[8,8,32,256]{3,2,1,0:T(8,128)(2,1)} %get-tuple-element.43), channel_id=1, replica_groups=mesh['z'=8,'g'=8,'mp'=4] {'g'}, dimensions={0} | all-to-all | bytes 2097152 | tf_op jit(solution)/shard_map/all_to_all | solution.py:438
  193.0 4.4 %gather_up.1 = bf16[8,4,32,256]{3,2,1,0:T(8,128)(2,1)} custom-call(s32[128]{0:T(128)} %reshape.22.ids_ref, s32[3]{0:T(128)} %pad_add_fusion.me_ref, bf16[8,8,32,256]{3,2,1,0:T(8,128)(2,1)} %all_to_all.25.got_ref), custom_call_target="tpu_custom_call" | custom-call | tf_op jit(solution)/shard_map/gather_up/pallas_call | solution.py:311
  197.4 5.6 %all-to-all-start.4 = ((bf16[8,4,32,256]{3,2,1,0:T(8,128)(2,1)}), bf16[8,4,32,256]{3,2,1,0:T(8,128)(2,1)S(1)}, u32[]{:S(2)}, u32[]{:S(2)}) async-start(bf16[8,4,32,256]{3,2,1,0:T(8,128)(2,1)} %gather_up.1), calls=%async_computation.5 | async-start | bytes 1048576 | tf_op jit(solution)/shard_map/all_to_all | solution.py:438
  206.2 6.2 %through_down.1 = (bf16[512,256]{1,0:T(8,128)(2,1)}, bf16[512,256]{1,0:T(8,128)(2,1)}, bf16[512,256]{1,0:T(8,128)(2,1)}, bf16[512,256]{1,0:T(8,128)(2,1)}, bf16[...) custom-call(s32[128]{0:T(128)} %fusion.ids_ref, ...), custom_call_target="tpu_custom_call" | custom-call | tf_op jit(solution)/shard_map/through_down/pallas_call | solution.py:249
  224.0 6.3 %collective-permute-start.39 = (bf16[512,256]{1,0:T(8,128)(2,1)}, bf16[512,256]{1,0:T(8,128)(2,1)S(1)}, u32[]{:S(2)}, u32[]{:S(2)}) collective-permute-start(bf16[512,256]{1,0:T(8,128)(2,1)} %get-tuple-element.42), channel_id=1, source_target_pairs={{0,4},{4,8},{8,12},{12,16},{16,20},{20,24},{24,28},{28,0},{1,5},{5... | collective-permute-start | bytes 786440 | tf_op jit(solution)/shard_map/ppermute | solution.py:423
  234.0 3.2 %collective-permute-start.41 = (bf16[4,32,256]{2,1,0:T(8,128)(2,1)}, bf16[4,32,256]{2,1,0:T(8,128)(2,1)}, u32[]{:S(2)}, u32[]{:S(2)}) collective-permute-start(bf16[4,32,256]{2,1,0:T(8,128)(2,1)} %get-tuple-element.60), channel_id=1, source_target_pairs={{0,8},{4,12},{8,16},{12,20},{16,24},{20,28},{24,0},{28,4},{1,9},{5... | collective-permute-start | bytes 196616 | tf_op jit(solution)/shard_map/ppermute | solution.py:423
  238.0 3.6 %collective-permute-done.39.refs_12_ = bf16[512,256]{1,0:T(8,128)(2,1)S(1)} collective-permute-done((bf16[512,256]{1,0:T(8,128)(2,1)}, bf16[512,256]{1,0:T(8,128)(2,1)S(1)}, u32[]{:S(2)}, u32[]{:S(2)}) %collective-permute-start.39) | collective-permute-done | bytes 262176 | tf_op jit(solution)/shard_map/ppermute | solution.py:423
  242.3 9.9 %input_gradient.1 = bf16[512,2048]{1,0:T(8,128)(2,1)} custom-call(s32[3]{0:T(128)} %pad_add_fusion.me_ref, bf16[512,256]{1,0:T(8,128)(2,1)} %refs_0_.1, bf16[512,256]{1,0:T(8,128)(2,1)} %copy-done.10, bf16[512,256]{1,0:T(8,128)(2,1)} %copy-done.11, bf16[512,256]{1,0:T(8,128)(2,1)} %copy-done.12, bf16[2048,1024]{1,0:T(8,128)(2,1)} %refs_4_.1, ...), custom_call_target="tpu_custom_call" | custom-call | tf_op jit(solution)/shard_map/input_gradient/pallas_call | solution.py:345
  252.2 4.0 %collective-permute-start.42 = (bf16[4,32,256]{2,1,0:T(8,128)(2,1)S(1)}, bf16[4,32,256]{2,1,0:T(8,128)(2,1)S(1)}, u32[]{:S(2)}, u32[]{:S(2)}) collective-permute-start(bf16[4,32,256]{2,1,0:T(8,128)(2,1)S(1)} %get-tuple-element.59), channel_id=1, source_target_pairs={{0,12},{4,16},{8,20},{12,24},{16,28},{20,0},{24,4},{28,8},{1,13},{... | collective-permute-start | bytes 196616 | tf_op jit(solution)/shard_map/ppermute | solution.py:423
  (195 shorter events, 92.4 us)
Async XLA Ops:
  7.2 123.6 %all-gather.2.cloned.1.call-start = ((), (), s32[]{:S(2)}) async-start(), calls=%async_computation.6 | async-start | bytes 4718592 | tf_op jit(solution)/shard_map/all_gather | solution.py:453
  27.0 25.8 %all-to-all-start.1 = ((bf16[8,4,32,256]{3,2,1,0:T(8,128)(2,1)}), bf16[8,4,32,256]{3,2,1,0:T(8,128)(2,1)S(1)}, u32[]{:S(2)}, u32[]{:S(2)}) async-start(bf16[8,4,32,256]{3,2,1,0:T(8,128)(2,1)} %broadcast_in_dim.10), calls=%async_computation.1 | async-start | bytes 1048576 | tf_op jit(solution)/shard_map/all_to_all | solution.py:438
  57.9 21.6 %all-to-all-start.2 = ((bf16[8,8,32,256]{3,2,1,0:T(8,128)(2,1)}), bf16[8,8,32,256]{3,2,1,0:T(8,128)(2,1)S(1)}, u32[]{:S(2)}, u32[]{:S(2)}) async-start(bf16[8,8,32,256]{3,2,1,0:T(8,128)(2,1)} %select_up.1), calls=%async_computation.2 | async-start | bytes 2097152 | tf_op jit(solution)/shard_map/all_to_all | solution.py:438
  66.8 163.5 %reduce-scatter.2.cloned.1.call-start = ((), (), s32[]{:S(2)}) async-start(), calls=%async_computation.7 | async-start | bytes 4718592 | tf_op jit(solution)/shard_map/reduce_scatter | solution.py:483
  68.2 18.4 %collective-permute-start.7 = (bf16[512,256]{1,0:T(8,128)(2,1)}, bf16[512,256]{1,0:T(8,128)(2,1)S(1)}, u32[]{:S(2)}, u32[]{:S(2)}) collective-permute-start(bf16[512,256]{1,0:T(8,128)(2,1)} %get-tuple-element.53), channel_id=1, source_target_pairs={{0,4},{4,8},{8,12},{12,16},{16,20},{20,24},{24,28},{28,0},{1,5},{5... | collective-permute-start | bytes 786440 | tf_op jit(solution)/shard_map/ppermute | solution.py:423
  69.4 22.0 %collective-permute-start.8 = (bf16[512,256]{1,0:T(8,128)(2,1)}, bf16[512,256]{1,0:T(8,128)(2,1)}, u32[]{:S(2)}, u32[]{:S(2)}) collective-permute-start(bf16[512,256]{1,0:T(8,128)(2,1)} %get-tuple-element.52), channel_id=1, source_target_pairs={{0,8},{4,12},{8,16},{12,20},{16,24},{20,28},{24,0},{28,4},{1,9},{5... | collective-permute-start | bytes 786440 | tf_op jit(solution)/shard_map/ppermute | solution.py:423
  91.3 14.8 %collective-permute-start.10 = (bf16[512,256]{1,0:T(8,128)(2,1)}, bf16[512,256]{1,0:T(8,128)(2,1)S(1)}, u32[]{:S(2)}, u32[]{:S(2)}) collective-permute-start(bf16[512,256]{1,0:T(8,128)(2,1)} %get-tuple-element.50), channel_id=1, source_target_pairs={{0,16},{4,20},{8,24},{12,28},{16,0},{20,4},{24,8},{28,12},{1,17},{... | collective-permute-start | bytes 786440 | tf_op jit(solution)/shard_map/ppermute | solution.py:423
  91.4 17.6 %collective-permute-start.11 = (bf16[512,256]{1,0:T(8,128)(2,1)}, bf16[512,256]{1,0:T(8,128)(2,1)S(1)}, u32[]{:S(2)}, u32[]{:S(2)}) collective-permute-start(bf16[512,256]{1,0:T(8,128)(2,1)} %get-tuple-element.49), channel_id=1, source_target_pairs={{0,20},{4,24},{8,28},{12,0},{16,4},{20,8},{24,12},{28,16},{1,21},{... | collective-permute-start | bytes 786440 | tf_op jit(solution)/shard_map/ppermute | solution.py:423
  91.7 22.9 %collective-permute-start.12 = (bf16[512,256]{1,0:T(8,128)(2,1)}, bf16[512,256]{1,0:T(8,128)(2,1)S(1)}, u32[]{:S(2)}, u32[]{:S(2)}) collective-permute-start(bf16[512,256]{1,0:T(8,128)(2,1)} %get-tuple-element.48), channel_id=1, source_target_pairs={{0,24},{4,28},{8,0},{12,4},{16,8},{20,12},{24,16},{28,20},{1,25},{... | collective-permute-start | bytes 786440 | tf_op jit(solution)/shard_map/ppermute | solution.py:423
  92.9 23.0 %collective-permute-start.13 = (bf16[512,256]{1,0:T(8,128)(2,1)}, bf16[512,256]{1,0:T(8,128)(2,1)}, u32[]{:S(2)}, u32[]{:S(2)}) collective-permute-start(bf16[512,256]{1,0:T(8,128)(2,1)} %get-tuple-element.47), channel_id=1, source_target_pairs={{0,28},{4,0},{8,4},{12,8},{16,12},{20,16},{24,20},{28,24},{1,29},{... | collective-permute-start | bytes 786440 | tf_op jit(solution)/shard_map/ppermute | solution.py:423
  97.5 18.4 %collective-permute-start.26 = (bf16[4,32,128]{2,1,0:T(8,128)(2,1)S(1)}, bf16[4,32,128]{2,1,0:T(8,128)(2,1)S(1)}, u32[]{:S(2)}, u32[]{:S(2)}) collective-permute-start(bf16[4,32,128]{2,1,0:T(8,128)(2,1)S(1)} %multiply_convert_fusion.refs_0_), channel_id=1, source_target_pairs={{0,4},{4,8},{8,12},{12,16},{16,20},{20,24},{24,28},{28,0},{1,5},{5... | collective-permute-start | bytes 98312 | tf_op jit(solution)/shard_map/ppermute | solution.py:423
  136.7 17.6 %all-to-all-start = ((f32[8,4,32,128]{3,2,1,0:T(8,128)}), f32[8,4,32,128]{3,2,1,0:T(8,128)S(1)}, u32[]{:S(2)}, u32[]{:S(2)}) async-start(f32[8,4,32,128]{3,2,1,0:T(8,128)} %rank_part.1), calls=%async_computation | async-start | bytes 1048576 | tf_op jit(solution)/shard_map/all_to_all | solution.py:438
  154.4 14.5 %collective-permute-start.17 = (bf16[512,256]{1,0:T(8,128)(2,1)S(1)}, bf16[512,256]{1,0:T(8,128)(2,1)S(1)}, u32[]{:S(2)}, u32[]{:S(2)}) collective-permute-start(bf16[512,256]{1,0:T(8,128)(2,1)S(1)} %get-tuple-element.44), channel_id=1, source_target_pairs={{0,1},{1,2},{2,3},{3,0},{4,5},{5,6},{6,7},{7,4},{8,9},{9,10},{10,1... | collective-permute-start | bytes 786440 | tf_op jit(solution)/shard_map/ppermute | solution.py:423
  154.4 16.4 %collective-permute-start.16 = (f32[4,32,128]{2,1,0:T(8,128)S(1)}, f32[4,32,128]{2,1,0:T(8,128)S(1)}, u32[]{:S(2)}, u32[]{:S(2)}) collective-permute-start(f32[4,32,128]{2,1,0:T(8,128)S(1)} %reduce_sum.18), channel_id=1, source_target_pairs={{0,3},{1,0},{2,1},{3,2},{4,7},{5,4},{6,5},{7,6},{8,11},{9,8},{10,9... | collective-permute-start | bytes 196616 | tf_op jit(solution)/shard_map/ppermute | solution.py:423
  157.1 13.7 %collective-permute-start.15 = (f32[4,32,128]{2,1,0:T(8,128)S(1)}, f32[4,32,128]{2,1,0:T(8,128)S(1)}, u32[]{:S(2)}, u32[]{:S(2)}) collective-permute-start(f32[4,32,128]{2,1,0:T(8,128)S(1)} %reduce_sum.18), channel_id=1, source_target_pairs={{0,2},{1,3},{2,0},{3,1},{4,6},{5,7},{6,4},{7,5},{8,10},{9,11},{10,... | collective-permute-start | bytes 196616 | tf_op jit(solution)/shard_map/ppermute | solution.py:423
  197.4 62.2 %all-to-all-start.4 = ((bf16[8,4,32,256]{3,2,1,0:T(8,128)(2,1)}), bf16[8,4,32,256]{3,2,1,0:T(8,128)(2,1)S(1)}, u32[]{:S(2)}, u32[]{:S(2)}) async-start(bf16[8,4,32,256]{3,2,1,0:T(8,128)(2,1)} %gather_up.1), calls=%async_computation.5 | async-start | bytes 1048576 | tf_op jit(solution)/shard_map/all_to_all | solution.py:438
  203.6 13.8 %collective-permute-start.21 = (bf16[512,256]{1,0:T(8,128)(2,1)S(1)}, bf16[512,256]{1,0:T(8,128)(2,1)S(1)}, u32[]{:S(2)}, u32[]{:S(2)}) collective-permute-start(bf16[512,256]{1,0:T(8,128)(2,1)S(1)} %copy-done.1), channel_id=1, source_target_pairs={{0,2},{1,3},{2,0},{3,1},{4,6},{5,7},{6,4},{7,5},{8,10},{9,11},{10,... | collective-permute-start | bytes 786440 | tf_op jit(solution)/shard_map/ppermute | solution.py:423
  216.0 16.1 %collective-permute-start.35 = (bf16[512,256]{1,0:T(8,128)(2,1)}, bf16[512,256]{1,0:T(8,128)(2,1)S(1)}, u32[]{:S(2)}, u32[]{:S(2)}) collective-permute-start(bf16[512,256]{1,0:T(8,128)(2,1)} %get-tuple-element.38), channel_id=1, source_target_pairs={{0,20},{4,24},{8,28},{12,0},{16,4},{20,8},{24,12},{28,16},{1,21},{... | collective-permute-start | bytes 786440 | tf_op jit(solution)/shard_map/ppermute | solution.py:423
  217.4 16.7 %collective-permute-start.36 = (bf16[512,256]{1,0:T(8,128)(2,1)}, bf16[512,256]{1,0:T(8,128)(2,1)S(1)}, u32[]{:S(2)}, u32[]{:S(2)}) collective-permute-start(bf16[512,256]{1,0:T(8,128)(2,1)} %get-tuple-element.39), channel_id=1, source_target_pairs={{0,16},{4,20},{8,24},{12,28},{16,0},{20,4},{24,8},{28,12},{1,17},{... | collective-permute-start | bytes 786440 | tf_op jit(solution)/shard_map/ppermute | solution.py:423
  219.2 18.2 %collective-permute-start.37 = (bf16[512,256]{1,0:T(8,128)(2,1)}, bf16[512,256]{1,0:T(8,128)(2,1)S(1)}, u32[]{:S(2)}, u32[]{:S(2)}) collective-permute-start(bf16[512,256]{1,0:T(8,128)(2,1)} %get-tuple-element.40), channel_id=1, source_target_pairs={{0,12},{4,16},{8,20},{12,24},{16,28},{20,0},{24,4},{28,8},{1,13},{... | collective-permute-start | bytes 786440 | tf_op jit(solution)/shard_map/ppermute | solution.py:423
  223.1 14.8 %collective-permute-start.38 = (bf16[512,256]{1,0:T(8,128)(2,1)}, bf16[512,256]{1,0:T(8,128)(2,1)S(1)}, u32[]{:S(2)}, u32[]{:S(2)}) collective-permute-start(bf16[512,256]{1,0:T(8,128)(2,1)} %get-tuple-element.41), channel_id=1, source_target_pairs={{0,8},{4,12},{8,16},{12,20},{16,24},{20,28},{24,0},{28,4},{1,9},{5... | collective-permute-start | bytes 786440 | tf_op jit(solution)/shard_map/ppermute | solution.py:423
  224.0 17.6 %collective-permute-start.39 = (bf16[512,256]{1,0:T(8,128)(2,1)}, bf16[512,256]{1,0:T(8,128)(2,1)S(1)}, u32[]{:S(2)}, u32[]{:S(2)}) collective-permute-start(bf16[512,256]{1,0:T(8,128)(2,1)} %get-tuple-element.42), channel_id=1, source_target_pairs={{0,4},{4,8},{8,12},{12,16},{16,20},{20,24},{24,28},{28,0},{1,5},{5... | collective-permute-start | bytes 786440 | tf_op jit(solution)/shard_map/ppermute | solution.py:423
  232.1 25.4 %collective-permute-start.40 = (bf16[4,32,256]{2,1,0:T(8,128)(2,1)}, bf16[4,32,256]{2,1,0:T(8,128)(2,1)S(1)}, u32[]{:S(2)}, u32[]{:S(2)}) collective-permute-start(bf16[4,32,256]{2,1,0:T(8,128)(2,1)} %get-tuple-element.61), channel_id=1, source_target_pairs={{0,4},{4,8},{8,12},{12,16},{16,20},{20,24},{24,28},{28,0},{1,5},{5... | collective-permute-start | bytes 196616 | tf_op jit(solution)/shard_map/ppermute | solution.py:423
  234.0 24.1 %collective-permute-start.41 = (bf16[4,32,256]{2,1,0:T(8,128)(2,1)}, bf16[4,32,256]{2,1,0:T(8,128)(2,1)}, u32[]{:S(2)}, u32[]{:S(2)}) collective-permute-start(bf16[4,32,256]{2,1,0:T(8,128)(2,1)} %get-tuple-element.60), channel_id=1, source_target_pairs={{0,8},{4,12},{8,16},{12,20},{16,24},{20,28},{24,0},{28,4},{1,9},{5... | collective-permute-start | bytes 196616 | tf_op jit(solution)/shard_map/ppermute | solution.py:423
  (71 other events, 610.0 us)
Sparse Core Ops, SparseCore 0:
  25.5 63.1 all-gather.1
  129.7 52.4 reduce-scatter.1

commit v2 on v1

--- a/solution.py
+++ b/solution.py
@@ -63,8 +63,16 @@
     pltpu.make_async_copy(refs[0], stack.at[k], sems.at[k]).wait()
 
 
+def divide(x, n):
+    return x >> (n.bit_length() - 1) if n & (n - 1) == 0 else lax.div(x, n)
+
+
+def remainder(x, n):
+    return x & (n - 1) if n & (n - 1) == 0 else lax.rem(x, n)
+
+
 def back(me, k, size):
-    return lax.rem(me - k + size, size)
+    return remainder(me - k + size, size)
 
 
 def select_up(ids_all, me, gathered, plane):
@@ -76,13 +84,13 @@
 
         def step(b, carry):
             number = ids_ref[b]
-            owner = lax.div(number, owned)
-
-            @pl.when(lax.rem(owner, plane) == my_g)
+            owner = divide(number, owned)
+
+            @pl.when(remainder(owner, plane) == my_g)
             def _():
-                z = lax.div(owner, plane)
-                dest = back(my_g, lax.div(b, blocks), plane)
-                out_ref[dest, z] = all_ref[z, lax.rem(number, owned)]
+                z = divide(owner, plane)
+                dest = back(my_g, divide(b, blocks), plane)
+                out_ref[dest, z] = all_ref[z, remainder(number, owned)]
 
             return carry
 
@@ -100,8 +108,8 @@
 def up_rows(ids_ref, slots_ref, q, owned, plane):
     rows = []
     for i in range(QUAD):
-        owner = ids_ref[q * QUAD + i] // owned
-        rows.append(slots_ref[owner % plane, owner // plane])
+        owner = divide(ids_ref[q * QUAD + i], owned)
+        rows.append(slots_ref[remainder(owner, plane), divide(owner, plane)])
     return jnp.concatenate(rows, axis=0)
 
 
@@ -203,7 +211,7 @@
             for q in range(quads):
                 down = table_rows(ids_ref, table_ref, k * blocks + q * QUAD)
                 got = dot_nt(stack[k, q * span : (q + 1) * span, :], down)
-                out_ref[dest, q] = fold(got, mask, length)
+                out_ref[dest, q] = fold(got, mask, length).astype(bf)
             return carry
 
         lax.fori_loop(0, plane, step, 0)
@@ -212,7 +220,7 @@
         kernel,
         in_specs=[SMEM(), SMEM(), VMEM()] + [HBM()] * plane,
         out_specs=VMEM(),
-        out_shape=jax.ShapeDtypeStruct((plane, quads, length, QUAD * rank), f32),
+        out_shape=jax.ShapeDtypeStruct((plane, quads, length, QUAD * rank), bf),
         scratch_shapes=stacked(plane, tok[0]),
         name="rank_part",
     )(ids_all, me, table, *tok)
@@ -270,8 +278,8 @@
             out_ref[rows, :] = (base_ref[rows, :] + adapter_scale * dot_nn(wide, up)).astype(bf)
             got = (dot_tn(wide, cot_ref[rows, :]) * (adapter_scale / length)).astype(bf)
             for i in range(QUAD):
-                owner = ids_ref[q * QUAD + i] // owned
-                send_ref[owner % plane, owner // plane] = got[i * rank : (i + 1) * rank]
+                owner = divide(ids_ref[q * QUAD + i], owned)
+                send_ref[remainder(owner, plane), divide(owner, plane)] = got[i * rank : (i + 1) * rank]
 
     return pl.pallas_call(
         kernel,
@@ -295,12 +303,12 @@
 
         def step(b, carry):
             number = ids_ref[b]
-            owner = lax.div(number, owned)
-
-            @pl.when(lax.rem(owner, plane) == my_g)
+            owner = divide(number, owned)
+
+            @pl.when(remainder(owner, plane) == my_g)
             def _():
-                z, local = lax.div(owner, plane), lax.rem(number, owned)
-                acc[z, local] = acc[z, local] + got_ref[back(my_g, lax.div(b, blocks), plane), z].astype(f32)
+                z, local = divide(owner, plane), remainder(number, owned)
+                acc[z, local] = acc[z, local] + got_ref[back(my_g, divide(b, blocks), plane), z].astype(f32)
 
             return carry
 
@@ -328,19 +336,18 @@
 
     def kernel(me_ref, *refs):
         cot_refs, w_ref, thr_refs = refs[:parts], refs[parts], refs[parts + 1 : parts + 1 + plane]
-        out_ref, stack, sems = refs[parts + 1 + plane :]
+        out_ref, stack, sems, whole = refs[parts + 1 + plane :]
         i = pl.program_id(0)
 
         @pl.when(i == 0)
         def _():
             load(thr_refs, stack, sems)
+            for k in range(parts):
+                first = pl.multiple_of(back(me_ref[2], k, parts) * cols, cols)
+                whole[:, pl.ds(first, cols)] = cot_refs[k][...]
 
         loaded(thr_refs, stack, sems, i)
-        total = stack[i].astype(f32)
-        for k in range(parts):
-            first = pl.multiple_of(back(me_ref[2], k, parts) * cols, cols)
-            total = total + dot_nt(cot_refs[k][...], w_ref[:, pl.ds(first, cols)])
-        out_ref[...] = total.astype(bf)
+        out_ref[...] = (dot_nt(whole[...], w_ref[...]) + stack[i].astype(f32)).astype(bf)
 
     return pl.pallas_call(
         kernel,
@@ -351,7 +358,8 @@
             + [pl.BlockSpec((narrow, parts * cols), lambda i, me_ref: (ahead(i, me_ref), 0))]
             + [HBM()] * plane,
             out_specs=pl.BlockSpec((tokens, narrow), lambda i, me_ref: (0, ahead(i, me_ref))),
-            scratch_shapes=stacked(plane, through[0]),
+            scratch_shapes=stacked(plane, through[0])
+            + [pltpu.VMEM((tokens, parts * cols), bf)],
         ),
         out_shape=jax.ShapeDtypeStruct((tokens, plane * narrow), bf),
         name="input_gradient",
@@ -488,7 +496,7 @@
         grad_got.append(shift(part, "g", plane, k) if k else part)
     down_grad = down_gradient(me, grad_got)
 
-    ranks = mp_sum(jnp.sum(rank_parts, axis=0)).astype(bf)
+    ranks = mp_sum(jnp.sum(rank_parts.astype(f32), axis=0)).astype(bf)
 
     through_n = through_down(ids_row, me, table, rg_all)
     through = [through_n[0]]

time: 277 us -> 272 us (0.982)
  starting transfers between devices: 105 us -> 101 us
    ppermute x47, starting transfers between devices: 75.3 us -> 72.2 us  [shift(): return lax.ppermute(x, axis, [(i, (i + k) % size) for i in range(size)])]
  transfers between devices with their start and end apart: 53 -> 53, of which waited for: 22 -> 20; matrix products, arithmetic and copies ran while one was open for 6% -> 6% of each run, Pallas kernels for 16% -> 15%
where the time goes in v2:
time: 272 us; the launch traced here: 267 us
  starting transfers between devices  101 us (37%)
  waiting for transfers between devices  64 us (24%)
  Pallas kernels  47.2 us (17%)
  blocking collectives  18 us (7%)
  between operations  14.4 us (5%)
  local copies, waits for them, and re-layouts  11.1 us (4%)
  other arithmetic  6.07 us (2%)
  matrix products  5.84 us (2%)
    ppermute x47, starting transfers between devices, shift(): return lax.ppermute(x, axis, [(i, (i + k) % size) for i in range(size)])  72.2 us
    ppermute x47, waiting for transfers between devices, shift(): return lax.ppermute(x, axis, [(i, (i + k) % size) for i in range(size)])  36 us
    all_to_all x4, starting transfers between devices, exchange(): return lax.all_to_all(x, axis, split_axis=0, concat_axis=0, tiled=True)  28.5 us
    all_to_all x4, waiting for transfers between devices, exchange(): return lax.all_to_all(x, axis, split_axis=0, concat_axis=0, tiled=True)  27.9 us
    all_to_all x1, blocking collectives, exchange(): return lax.all_to_all(x, axis, split_axis=0, concat_axis=0, tiled=True)  18 us
    pallas_call x1, Pallas kernels, input_gradient(): pl.pallas_call(kernel, grid_spec=pltpu.PrefetchScalarGridSpec(num_scalar_...  9.87 us
    pallas_call x1, Pallas kernels, down_terms(): pl.pallas_call(kernel, in_specs=[SMEM(), SMEM()] + [HBM()] * (2 * plane),...  6.65 us
    pallas_call x1, Pallas kernels, through_down(): pl.pallas_call(kernel, in_specs=[SMEM(), SMEM(), VMEM()] + [HBM()] * plan...  6.19 us
  transfers between devices with their start and end apart: 53, of which 20 were waited for; matrix products, arithmetic and copies ran while one was open for 6% of the time, Pallas kernels for 15%

profile of v2, /device:TPU:37, one launch (start us, length us, event | category | flops | bytes accessed | tf_op | source)
XLA Modules:
  0.0 267.3 jit_solution(8268946781498536901)
XLA Ops:
  27.1 8.0 %all-to-all-start.1 = ((bf16[8,4,32,256]{3,2,1,0:T(8,128)(2,1)}), bf16[8,4,32,256]{3,2,1,0:T(8,128)(2,1)S(1)}, u32[]{:S(2)}, u32[]{:S(2)}) async-start(bf16[8,4,32,256]{3,2,1,0:T(8,128)(2,1)} %broadcast_in_dim.10), calls=%async_computation.1 | async-start | bytes 1048576 | tf_op jit(solution)/shard_map/all_to_all | solution.py:446
  35.7 17.1 %all-to-all-done.1.all_ref = bf16[8,4,32,256]{3,2,1,0:T(8,128)(2,1)S(1)} async-done(((bf16[8,4,32,256]{3,2,1,0:T(8,128)(2,1)}), bf16[8,4,32,256]{3,2,1,0:T(8,128)(2,1)S(1)}, u32[]{:S(2)}, u32[]{:S(2)}) %all-to-all-start.1) | async-done | bytes 524320 | tf_op jit(solution)/shard_map/all_to_all | solution.py:446
  53.6 3.7 %select_up.1 = bf16[8,8,32,256]{3,2,1,0:T(8,128)(2,1)} custom-call(s32[128]{0:T(128)} %reshape.22.ids_ref, s32[3]{0:T(128)} %pad_add_fusion.me_ref, bf16[8,4,32,256]{3,2,1,0:T(8,128)(2,1)} %copy-done.3), custom_call_target="tpu_custom_call" | custom-call | tf_op jit(solution)/shard_map/select_up/pallas_call | solution.py:99
  57.3 9.0 %all-to-all-start.2 = ((bf16[8,8,32,256]{3,2,1,0:T(8,128)(2,1)}), bf16[8,8,32,256]{3,2,1,0:T(8,128)(2,1)S(1)}, u32[]{:S(2)}, u32[]{:S(2)}) async-start(bf16[8,8,32,256]{3,2,1,0:T(8,128)(2,1)} %select_up.1), calls=%async_computation.2 | async-start | bytes 2097152 | tf_op jit(solution)/shard_map/all_to_all | solution.py:446
  68.4 10.6 %all-to-all-done.2.slots_ref = bf16[8,8,32,256]{3,2,1,0:T(8,128)(2,1)S(1)} async-done(((bf16[8,8,32,256]{3,2,1,0:T(8,128)(2,1)}), bf16[8,8,32,256]{3,2,1,0:T(8,128)(2,1)S(1)}, u32[]{:S(2)}, u32[]{:S(2)}) %all-to-all-start.2) | async-done | bytes 1048608 | tf_op jit(solution)/shard_map/all_to_all | solution.py:446
  82.1 2.9 %collective-permute-start.25 = (f32[4,32,128]{2,1,0:T(8,128)}, f32[4,32,128]{2,1,0:T(8,128)S(1)}, u32[]{:S(2)}, u32[]{:S(2)}) collective-permute-start(f32[4,32,128]{2,1,0:T(8,128)} %rank_grad_part.1), channel_id=1, source_target_pairs={{0,3},{1,0},{2,1},{3,2},{4,7},{5,4},{6,5},{7,6},{8,11},{9,8},{10,9... | collective-permute-start | bytes 196616 | tf_op jit(solution)/shard_map/ppermute | solution.py:431
  85.9 3.9 %collective-permute-start.11 = (bf16[512,256]{1,0:T(8,128)(2,1)}, bf16[512,256]{1,0:T(8,128)(2,1)S(1)}, u32[]{:S(2)}, u32[]{:S(2)}) collective-permute-start(bf16[512,256]{1,0:T(8,128)(2,1)} %get-tuple-element.49), channel_id=1, source_target_pairs={{0,20},{4,24},{8,28},{12,0},{16,4},{20,8},{24,12},{28,16},{1,21},{... | collective-permute-start | bytes 786440 | tf_op jit(solution)/shard_map/ppermute | solution.py:431
  96.6 8.5 %collective-permute-done.11.refs_5_.refs_13_ = bf16[512,256]{1,0:T(8,128)(2,1)S(1)} collective-permute-done((bf16[512,256]{1,0:T(8,128)(2,1)}, bf16[512,256]{1,0:T(8,128)(2,1)S(1)}, u32[]{:S(2)}, u32[]{:S(2)}) %collective-permute-start.11) | collective-permute-done | bytes 262176 | tf_op jit(solution)/shard_map/ppermute | solution.py:431
  112.6 5.5 %collective-permute-start.28 = (bf16[4,32,128]{2,1,0:T(8,128)(2,1)S(1)}, bf16[4,32,128]{2,1,0:T(8,128)(2,1)S(1)}, u32[]{:S(2)}, u32[]{:S(2)}) collective-permute-start(bf16[4,32,128]{2,1,0:T(8,128)(2,1)S(1)} %multiply_convert_fusion.refs_0_), channel_id=1, source_target_pairs={{0,12},{4,16},{8,20},{12,24},{16,28},{20,0},{24,4},{28,8},{1,13},{... | collective-permute-start | bytes 98312 | tf_op jit(solution)/shard_map/ppermute | solution.py:431
  122.6 6.6 %down_terms.1 = bf16[256,32,256]{2,1,0:T(8,128)(2,1)} custom-call(s32[128]{0:T(128)} %reshape.22.ids_ref, s32[3]{0:T(128)} %pad_add_fusion.me_ref, bf16[4,32,128]{2,1,0:T(8,128)(2,1)} %copy-done.10, bf16[4,32,128]{2,1,0:T(8,128)(2,1)} %copy-done.27, bf16[4,32,128]{2,1,0:T(8,128)(2,1)} %copy-done.26, bf16[4,32,128]{2,1,0:T(8,128)(2,1)} %copy-done.25, ...), custom_call_target="tpu_custom_call" | custom-call | tf_op jit(solution)/shard_map/down_terms/pallas_call | solution.py:178
  129.3 5.8 %fusion.5 = f32[512,1024]{1,0:T(8,128)} fusion(bf16[512,2048]{1,0:T(8,128)(2,1)S(1)} %copy-done.2, bf16[2048,1024]{1,0:T(8,128)(2,1)} %refs_4_.1), kind=kOutput, calls=%fused_computation.43 | convolution fusion | flops 2147483648 | bytes 8388608 | tf_op jit(solution)/shard_map/dot_general | solution.py:472
  135.7 6.0 %rank_part.1 = bf16[8,4,32,128]{3,2,1,0:T(8,128)(2,1)} custom-call(s32[128]{0:T(128)} %fusion.ids_ref, s32[3]{0:T(128)} %pad_add_fusion.me_ref, bf16[256,32,256]{2,1,0:T(8,128)(2,1)} %all-gather.2.cloned.1.call-done.table_ref, bf16[512,256]{1,0:T(8,128)(2,1)} %get-tuple-element.54.refs_0_.refs_8_, bf16[512,256]{1,0:T(8,128)(2,1)} %collective-permute-done.7.refs_1_.refs_9_, ...), custom_call_target="tpu_custom_call" | custom-call | tf_op jit(solution)/shard_map/rank_part/pallas_call | solution.py:219
  141.7 6.2 %all-to-all-start = ((bf16[8,4,32,128]{3,2,1,0:T(8,128)(2,1)}), bf16[8,4,32,128]{3,2,1,0:T(8,128)(2,1)S(1)}, u32[]{:S(2)}, u32[]{:S(2)}) async-start(bf16[8,4,32,128]{3,2,1,0:T(8,128)(2,1)} %rank_part.1), calls=%async_computation | async-start | bytes 524288 | tf_op jit(solution)/shard_map/all_to_all | solution.py:446
  157.2 6.0 %collective-permute-done.18 = bf16[512,256]{1,0:T(8,128)(2,1)} collective-permute-done((bf16[512,256]{1,0:T(8,128)(2,1)S(1)}, bf16[512,256]{1,0:T(8,128)(2,1)}, u32[]{:S(2)}, u32[]{:S(2)}) %collective-permute-start.18) | collective-permute-done | bytes 262176 | tf_op jit(solution)/shard_map/ppermute | solution.py:431
  170.1 18.0 %all_to_all.25.got_ref = bf16[8,8,32,256]{3,2,1,0:T(8,128)(2,1)} all-to-all(bf16[8,8,32,256]{3,2,1,0:T(8,128)(2,1)} %get-tuple-element.43), channel_id=1, replica_groups=mesh['z'=8,'g'=8,'mp'=4] {'g'}, dimensions={0} | all-to-all | bytes 2097152 | tf_op jit(solution)/shard_map/all_to_all | solution.py:446
  188.1 3.8 %gather_up.1 = bf16[8,4,32,256]{3,2,1,0:T(8,128)(2,1)} custom-call(s32[128]{0:T(128)} %reshape.22.ids_ref, s32[3]{0:T(128)} %pad_add_fusion.me_ref, bf16[8,8,32,256]{3,2,1,0:T(8,128)(2,1)} %all_to_all.25.got_ref), custom_call_target="tpu_custom_call" | custom-call | tf_op jit(solution)/shard_map/gather_up/pallas_call | solution.py:319
  191.9 5.3 %all-to-all-start.4 = ((bf16[8,4,32,256]{3,2,1,0:T(8,128)(2,1)}), bf16[8,4,32,256]{3,2,1,0:T(8,128)(2,1)S(1)}, u32[]{:S(2)}, u32[]{:S(2)}) async-start(bf16[8,4,32,256]{3,2,1,0:T(8,128)(2,1)} %gather_up.1), calls=%async_computation.5 | async-start | bytes 1048576 | tf_op jit(solution)/shard_map/all_to_all | solution.py:446
  197.2 2.8 %collective-permute-start.22 = (bf16[512,256]{1,0:T(8,128)(2,1)S(1)}, bf16[512,256]{1,0:T(8,128)(2,1)S(1)}, u32[]{:S(2)}, u32[]{:S(2)}) collective-permute-start(bf16[512,256]{1,0:T(8,128)(2,1)S(1)} %copy-done.1), channel_id=1, source_target_pairs={{0,3},{1,0},{2,1},{3,2},{4,7},{5,4},{6,5},{7,6},{8,11},{9,8},{10,9... | collective-permute-start | bytes 786440 | tf_op jit(solution)/shard_map/ppermute | solution.py:431
  200.7 6.2 %through_down.1 = (bf16[512,256]{1,0:T(8,128)(2,1)}, bf16[512,256]{1,0:T(8,128)(2,1)}, bf16[512,256]{1,0:T(8,128)(2,1)}, bf16[512,256]{1,0:T(8,128)(2,1)}, bf16[...) custom-call(s32[128]{0:T(128)} %fusion.ids_ref, ...), custom_call_target="tpu_custom_call" | custom-call | tf_op jit(solution)/shard_map/through_down/pallas_call | solution.py:257
  210.3 3.3 %collective-permute-start.35 = (bf16[512,256]{1,0:T(8,128)(2,1)}, bf16[512,256]{1,0:T(8,128)(2,1)S(1)}, u32[]{:S(2)}, u32[]{:S(2)}) collective-permute-start(bf16[512,256]{1,0:T(8,128)(2,1)} %get-tuple-element.38), channel_id=1, source_target_pairs={{0,20},{4,24},{8,28},{12,0},{16,4},{20,8},{24,12},{28,16},{1,21},{... | collective-permute-start | bytes 786440 | tf_op jit(solution)/shard_map/ppermute | solution.py:431
  218.8 5.7 %collective-permute-start.39 = (bf16[512,256]{1,0:T(8,128)(2,1)}, bf16[512,256]{1,0:T(8,128)(2,1)S(1)}, u32[]{:S(2)}, u32[]{:S(2)}) collective-permute-start(bf16[512,256]{1,0:T(8,128)(2,1)} %get-tuple-element.42), channel_id=1, source_target_pairs={{0,4},{4,8},{8,12},{12,16},{16,20},{20,24},{24,28},{28,0},{1,5},{5... | collective-permute-start | bytes 786440 | tf_op jit(solution)/shard_map/ppermute | solution.py:431
  226.4 3.6 %collective-permute-start.45 = (bf16[4,32,256]{2,1,0:T(8,128)(2,1)}, bf16[4,32,256]{2,1,0:T(8,128)(2,1)}, u32[]{:S(2)}, u32[]{:S(2)}) collective-permute-start(bf16[4,32,256]{2,1,0:T(8,128)(2,1)} %get-tuple-element.56), channel_id=1, source_target_pairs={{0,24},{4,28},{8,0},{12,4},{16,8},{20,12},{24,16},{28,20},{1,25},{... | collective-permute-start | bytes 196616 | tf_op jit(solution)/shard_map/ppermute | solution.py:431
  236.6 9.9 %input_gradient.1 = bf16[512,2048]{1,0:T(8,128)(2,1)} custom-call(s32[3]{0:T(128)} %pad_add_fusion.me_ref, bf16[512,256]{1,0:T(8,128)(2,1)} %refs_0_.1, bf16[512,256]{1,0:T(8,128)(2,1)} %copy-done.13, bf16[512,256]{1,0:T(8,128)(2,1)} %copy-done.12, bf16[512,256]{1,0:T(8,128)(2,1)} %copy-done.11, bf16[2048,1024]{1,0:T(8,128)(2,1)} %refs_4_.1, ...), custom_call_target="tpu_custom_call" | custom-call | tf_op jit(solution)/shard_map/input_gradient/pallas_call | solution.py:352
  246.4 3.5 %collective-permute-start.44 = (bf16[4,32,256]{2,1,0:T(8,128)(2,1)S(1)}, bf16[4,32,256]{2,1,0:T(8,128)(2,1)S(1)}, u32[]{:S(2)}, u32[]{:S(2)}) collective-permute-start(bf16[4,32,256]{2,1,0:T(8,128)(2,1)S(1)} %get-tuple-element.57), channel_id=1, source_target_pairs={{0,20},{4,24},{8,28},{12,0},{16,4},{20,8},{24,12},{28,16},{1,21},{... | collective-permute-start | bytes 196616 | tf_op jit(solution)/shard_map/ppermute | solution.py:431
  (197 shorter events, 91.0 us)
Async XLA Ops:
  7.2 128.6 %all-gather.2.cloned.1.call-start = ((), (), s32[]{:S(2)}) async-start(), calls=%async_computation.6 | async-start | bytes 4718592 | tf_op jit(solution)/shard_map/all_gather | solution.py:461
  27.1 25.8 %all-to-all-start.1 = ((bf16[8,4,32,256]{3,2,1,0:T(8,128)(2,1)}), bf16[8,4,32,256]{3,2,1,0:T(8,128)(2,1)S(1)}, u32[]{:S(2)}, u32[]{:S(2)}) async-start(bf16[8,4,32,256]{3,2,1,0:T(8,128)(2,1)} %broadcast_in_dim.10), calls=%async_computation.1 | async-start | bytes 1048576 | tf_op jit(solution)/shard_map/all_to_all | solution.py:446
  57.3 21.6 %all-to-all-start.2 = ((bf16[8,8,32,256]{3,2,1,0:T(8,128)(2,1)}), bf16[8,8,32,256]{3,2,1,0:T(8,128)(2,1)S(1)}, u32[]{:S(2)}, u32[]{:S(2)}) async-start(bf16[8,8,32,256]{3,2,1,0:T(8,128)(2,1)} %select_up.1), calls=%async_computation.2 | async-start | bytes 2097152 | tf_op jit(solution)/shard_map/all_to_all | solution.py:446
  66.3 158.2 %reduce-scatter.2.cloned.1.call-start = ((), (), s32[]{:S(2)}) async-start(), calls=%async_computation.7 | async-start | bytes 4718592 | tf_op jit(solution)/shard_map/reduce_scatter | solution.py:491
  67.7 18.2 %collective-permute-start.13 = (bf16[512,256]{1,0:T(8,128)(2,1)}, bf16[512,256]{1,0:T(8,128)(2,1)S(1)}, u32[]{:S(2)}, u32[]{:S(2)}) collective-permute-start(bf16[512,256]{1,0:T(8,128)(2,1)} %get-tuple-element.47), channel_id=1, source_target_pairs={{0,28},{4,0},{8,4},{12,8},{16,12},{20,16},{24,20},{28,24},{1,29},{... | collective-permute-start | bytes 786440 | tf_op jit(solution)/shard_map/ppermute | solution.py:431
  68.1 21.7 %collective-permute-start.12 = (bf16[512,256]{1,0:T(8,128)(2,1)}, bf16[512,256]{1,0:T(8,128)(2,1)}, u32[]{:S(2)}, u32[]{:S(2)}) collective-permute-start(bf16[512,256]{1,0:T(8,128)(2,1)} %get-tuple-element.48), channel_id=1, source_target_pairs={{0,24},{4,28},{8,0},{12,4},{16,8},{20,12},{24,16},{28,20},{1,25},{... | collective-permute-start | bytes 786440 | tf_op jit(solution)/shard_map/ppermute | solution.py:431
  85.9 19.1 %collective-permute-start.11 = (bf16[512,256]{1,0:T(8,128)(2,1)}, bf16[512,256]{1,0:T(8,128)(2,1)S(1)}, u32[]{:S(2)}, u32[]{:S(2)}) collective-permute-start(bf16[512,256]{1,0:T(8,128)(2,1)} %get-tuple-element.49), channel_id=1, source_target_pairs={{0,20},{4,24},{8,28},{12,0},{16,4},{20,8},{24,12},{28,16},{1,21},{... | collective-permute-start | bytes 786440 | tf_op jit(solution)/shard_map/ppermute | solution.py:431
  89.8 15.2 %collective-permute-start.10 = (bf16[512,256]{1,0:T(8,128)(2,1)}, bf16[512,256]{1,0:T(8,128)(2,1)S(1)}, u32[]{:S(2)}, u32[]{:S(2)}) collective-permute-start(bf16[512,256]{1,0:T(8,128)(2,1)} %get-tuple-element.50), channel_id=1, source_target_pairs={{0,16},{4,20},{8,24},{12,28},{16,0},{20,4},{24,8},{28,12},{1,17},{... | collective-permute-start | bytes 786440 | tf_op jit(solution)/shard_map/ppermute | solution.py:431
  91.6 17.2 %collective-permute-start.9 = (bf16[512,256]{1,0:T(8,128)(2,1)}, bf16[512,256]{1,0:T(8,128)(2,1)S(1)}, u32[]{:S(2)}, u32[]{:S(2)}) collective-permute-start(bf16[512,256]{1,0:T(8,128)(2,1)} %get-tuple-element.51), channel_id=1, source_target_pairs={{0,12},{4,16},{8,20},{12,24},{16,28},{20,0},{24,4},{28,8},{1,13},{... | collective-permute-start | bytes 786440 | tf_op jit(solution)/shard_map/ppermute | solution.py:431
  92.0 17.3 %collective-permute-start.8 = (bf16[512,256]{1,0:T(8,128)(2,1)}, bf16[512,256]{1,0:T(8,128)(2,1)S(1)}, u32[]{:S(2)}, u32[]{:S(2)}) collective-permute-start(bf16[512,256]{1,0:T(8,128)(2,1)} %get-tuple-element.52), channel_id=1, source_target_pairs={{0,8},{4,12},{8,16},{12,20},{16,24},{20,28},{24,0},{28,4},{1,9},{5... | collective-permute-start | bytes 786440 | tf_op jit(solution)/shard_map/ppermute | solution.py:431
  93.2 19.5 %collective-permute-start.7 = (bf16[512,256]{1,0:T(8,128)(2,1)}, bf16[512,256]{1,0:T(8,128)(2,1)}, u32[]{:S(2)}, u32[]{:S(2)}) collective-permute-start(bf16[512,256]{1,0:T(8,128)(2,1)} %get-tuple-element.53), channel_id=1, source_target_pairs={{0,4},{4,8},{8,12},{12,16},{16,20},{20,24},{24,28},{28,0},{1,5},{5... | collective-permute-start | bytes 786440 | tf_op jit(solution)/shard_map/ppermute | solution.py:431
  105.0 13.2 %collective-permute-start.32 = (bf16[4,32,128]{2,1,0:T(8,128)(2,1)S(1)}, bf16[4,32,128]{2,1,0:T(8,128)(2,1)S(1)}, u32[]{:S(2)}, u32[]{:S(2)}) collective-permute-start(bf16[4,32,128]{2,1,0:T(8,128)(2,1)S(1)} %multiply_convert_fusion.refs_0_), channel_id=1, source_target_pairs={{0,28},{4,0},{8,4},{12,8},{16,12},{20,16},{24,20},{28,24},{1,29},{... | collective-permute-start | bytes 98312 | tf_op jit(solution)/shard_map/ppermute | solution.py:431
  105.0 13.2 %collective-permute-start.31 = (bf16[4,32,128]{2,1,0:T(8,128)(2,1)S(1)}, bf16[4,32,128]{2,1,0:T(8,128)(2,1)S(1)}, u32[]{:S(2)}, u32[]{:S(2)}) collective-permute-start(bf16[4,32,128]{2,1,0:T(8,128)(2,1)S(1)} %multiply_convert_fusion.refs_0_), channel_id=1, source_target_pairs={{0,24},{4,28},{8,0},{12,4},{16,8},{20,12},{24,16},{28,20},{1,25},{... | collective-permute-start | bytes 98312 | tf_op jit(solution)/shard_map/ppermute | solution.py:431
  152.1 13.1 %collective-permute-start.16 = (f32[4,32,128]{2,1,0:T(8,128)S(1)}, f32[4,32,128]{2,1,0:T(8,128)S(1)}, u32[]{:S(2)}, u32[]{:S(2)}) collective-permute-start(f32[4,32,128]{2,1,0:T(8,128)S(1)} %convert_reduce_fusion.1), channel_id=1, source_target_pairs={{0,3},{1,0},{2,1},{3,2},{4,7},{5,4},{6,5},{7,6},{8,11},{9,8},{10,9... | collective-permute-start | bytes 196616 | tf_op jit(solution)/shard_map/ppermute | solution.py:431
  191.9 63.0 %all-to-all-start.4 = ((bf16[8,4,32,256]{3,2,1,0:T(8,128)(2,1)}), bf16[8,4,32,256]{3,2,1,0:T(8,128)(2,1)S(1)}, u32[]{:S(2)}, u32[]{:S(2)}) async-start(bf16[8,4,32,256]{3,2,1,0:T(8,128)(2,1)} %gather_up.1), calls=%async_computation.5 | async-start | bytes 1048576 | tf_op jit(solution)/shard_map/all_to_all | solution.py:446
  197.2 13.1 %collective-permute-start.22 = (bf16[512,256]{1,0:T(8,128)(2,1)S(1)}, bf16[512,256]{1,0:T(8,128)(2,1)S(1)}, u32[]{:S(2)}, u32[]{:S(2)}) collective-permute-start(bf16[512,256]{1,0:T(8,128)(2,1)S(1)} %copy-done.1), channel_id=1, source_target_pairs={{0,3},{1,0},{2,1},{3,2},{4,7},{5,4},{6,5},{7,6},{8,11},{9,8},{10,9... | collective-permute-start | bytes 786440 | tf_op jit(solution)/shard_map/ppermute | solution.py:431
  200.0 13.5 %collective-permute-start.21 = (bf16[512,256]{1,0:T(8,128)(2,1)S(1)}, bf16[512,256]{1,0:T(8,128)(2,1)S(1)}, u32[]{:S(2)}, u32[]{:S(2)}) collective-permute-start(bf16[512,256]{1,0:T(8,128)(2,1)S(1)} %copy-done.1), channel_id=1, source_target_pairs={{0,2},{1,3},{2,0},{3,1},{4,6},{5,7},{6,4},{7,5},{8,10},{9,11},{10,... | collective-permute-start | bytes 786440 | tf_op jit(solution)/shard_map/ppermute | solution.py:431
  200.1 15.1 %collective-permute-start.20 = (bf16[512,256]{1,0:T(8,128)(2,1)S(1)}, bf16[512,256]{1,0:T(8,128)(2,1)S(1)}, u32[]{:S(2)}, u32[]{:S(2)}) collective-permute-start(bf16[512,256]{1,0:T(8,128)(2,1)S(1)} %copy-done.1), channel_id=1, source_target_pairs={{0,1},{1,2},{2,3},{3,0},{4,5},{5,6},{6,7},{7,4},{8,9},{9,10},{10,1... | collective-permute-start | bytes 786440 | tf_op jit(solution)/shard_map/ppermute | solution.py:431
  210.3 16.1 %collective-permute-start.35 = (bf16[512,256]{1,0:T(8,128)(2,1)}, bf16[512,256]{1,0:T(8,128)(2,1)S(1)}, u32[]{:S(2)}, u32[]{:S(2)}) collective-permute-start(bf16[512,256]{1,0:T(8,128)(2,1)} %get-tuple-element.38), channel_id=1, source_target_pairs={{0,20},{4,24},{8,28},{12,0},{16,4},{20,8},{24,12},{28,16},{1,21},{... | collective-permute-start | bytes 786440 | tf_op jit(solution)/shard_map/ppermute | solution.py:431
  215.3 17.3 %collective-permute-start.37 = (bf16[512,256]{1,0:T(8,128)(2,1)}, bf16[512,256]{1,0:T(8,128)(2,1)S(1)}, u32[]{:S(2)}, u32[]{:S(2)}) collective-permute-start(bf16[512,256]{1,0:T(8,128)(2,1)} %get-tuple-element.40), channel_id=1, source_target_pairs={{0,12},{4,16},{8,20},{12,24},{16,28},{20,0},{24,4},{28,8},{1,13},{... | collective-permute-start | bytes 786440 | tf_op jit(solution)/shard_map/ppermute | solution.py:431
  218.0 15.2 %collective-permute-start.38 = (bf16[512,256]{1,0:T(8,128)(2,1)}, bf16[512,256]{1,0:T(8,128)(2,1)S(1)}, u32[]{:S(2)}, u32[]{:S(2)}) collective-permute-start(bf16[512,256]{1,0:T(8,128)(2,1)} %get-tuple-element.41), channel_id=1, source_target_pairs={{0,8},{4,12},{8,16},{12,20},{16,24},{20,28},{24,0},{28,4},{1,9},{5... | collective-permute-start | bytes 786440 | tf_op jit(solution)/shard_map/ppermute | solution.py:431
  218.8 17.0 %collective-permute-start.39 = (bf16[512,256]{1,0:T(8,128)(2,1)}, bf16[512,256]{1,0:T(8,128)(2,1)S(1)}, u32[]{:S(2)}, u32[]{:S(2)}) collective-permute-start(bf16[512,256]{1,0:T(8,128)(2,1)} %get-tuple-element.42), channel_id=1, source_target_pairs={{0,4},{4,8},{8,12},{12,16},{16,20},{20,24},{24,28},{28,0},{1,5},{5... | collective-permute-start | bytes 786440 | tf_op jit(solution)/shard_map/ppermute | solution.py:431
  226.3 26.6 %collective-permute-start.46 = (bf16[4,32,256]{2,1,0:T(8,128)(2,1)}, bf16[4,32,256]{2,1,0:T(8,128)(2,1)S(1)}, u32[]{:S(2)}, u32[]{:S(2)}) collective-permute-start(bf16[4,32,256]{2,1,0:T(8,128)(2,1)} %get-tuple-element.55), channel_id=1, source_target_pairs={{0,28},{4,0},{8,4},{12,8},{16,12},{20,16},{24,20},{28,24},{1,29},{... | collective-permute-start | bytes 196616 | tf_op jit(solution)/shard_map/ppermute | solution.py:431
  226.4 27.7 %collective-permute-start.45 = (bf16[4,32,256]{2,1,0:T(8,128)(2,1)}, bf16[4,32,256]{2,1,0:T(8,128)(2,1)}, u32[]{:S(2)}, u32[]{:S(2)}) collective-permute-start(bf16[4,32,256]{2,1,0:T(8,128)(2,1)} %get-tuple-element.56), channel_id=1, source_target_pairs={{0,24},{4,28},{8,0},{12,4},{16,8},{20,12},{24,16},{28,20},{1,25},{... | collective-permute-start | bytes 196616 | tf_op jit(solution)/shard_map/ppermute | solution.py:431
  (72 other events, 612.0 us)
Sparse Core Ops, SparseCore 0:
  25.5 63.1 all-gather.1
  129.4 50.8 reduce-scatter.1

commit v3 on v2

--- a/solution.py
+++ b/solution.py
@@ -326,44 +326,54 @@
     )(ids_all, me, got)
 
 
-def input_gradient(me, cots, weight, through):
-    parts, plane = len(cots), len(through)
+def base_gradient(me, cots, weight):
+    parts = len(cots)
     tokens, cols = cots[0].shape
-    narrow = through[0].shape[1]
-
-    def ahead(i, me_ref):
-        return lax.rem(me_ref[1] + i, plane)
+    features = weight.shape[0]
+    tile = 256
 
     def kernel(me_ref, *refs):
-        cot_refs, w_ref, thr_refs = refs[:parts], refs[parts], refs[parts + 1 : parts + 1 + plane]
-        out_ref, stack, sems, whole = refs[parts + 1 + plane :]
-        i = pl.program_id(0)
-
-        @pl.when(i == 0)
+        w_ref, out_ref, whole = refs[parts:]
+
+        @pl.when(pl.program_id(0) == 0)
         def _():
-            load(thr_refs, stack, sems)
             for k in range(parts):
                 first = pl.multiple_of(back(me_ref[2], k, parts) * cols, cols)
-                whole[:, pl.ds(first, cols)] = cot_refs[k][...]
-
-        loaded(thr_refs, stack, sems, i)
-        out_ref[...] = (dot_nt(whole[...], w_ref[...]) + stack[i].astype(f32)).astype(bf)
-
-    return pl.pallas_call(
-        kernel,
-        grid_spec=pltpu.PrefetchScalarGridSpec(
-            num_scalar_prefetch=1,
-            grid=(plane,),
-            in_specs=[pl.BlockSpec((tokens, cols), lambda i, me_ref: (0, 0))] * parts
-            + [pl.BlockSpec((narrow, parts * cols), lambda i, me_ref: (ahead(i, me_ref), 0))]
-            + [HBM()] * plane,
-            out_specs=pl.BlockSpec((tokens, narrow), lambda i, me_ref: (0, ahead(i, me_ref))),
-            scratch_shapes=stacked(plane, through[0])
-            + [pltpu.VMEM((tokens, parts * cols), bf)],
-        ),
+                whole[:, pl.ds(first, cols)] = refs[k][...]
+
+        out_ref[...] = dot_nt(whole[...], w_ref[...])
+
+    return pl.pallas_call(
+        kernel,
+        grid=(features // tile,),
+        in_specs=[SMEM()]
+        + [pl.BlockSpec((tokens, cols), lambda s: (0, 0))] * parts
+        + [pl.BlockSpec((tile, parts * cols), lambda s: (s, 0))],
+        out_specs=pl.BlockSpec((tokens, tile), lambda s: (0, s)),
+        out_shape=jax.ShapeDtypeStruct((tokens, features), f32),
+        scratch_shapes=[pltpu.VMEM((tokens, parts * cols), bf)],
+        name="base_gradient",
+    )(me, *cots, weight)
+
+
+def input_gradient(me, base, through):
+    plane = len(through)
+    tokens, narrow = through[0].shape
+
+    def kernel(me_ref, base_ref, *refs):
+        out_ref = refs[plane]
+        for k in range(plane):
+            first = pl.multiple_of(remainder(me_ref[1] + k, plane) * narrow, narrow)
+            cols = pl.ds(first, narrow)
+            out_ref[:, cols] = (base_ref[:, cols] + refs[k][...].astype(f32)).astype(bf)
+
+    return pl.pallas_call(
+        kernel,
+        in_specs=[SMEM()] + [VMEM()] * (plane + 1),
+        out_specs=VMEM(),
         out_shape=jax.ShapeDtypeStruct((tokens, plane * narrow), bf),
         name="input_gradient",
-    )(me, *cots, weight, *through)
+    )(me, base, *through)
 
 
 def pack_down(me, down, tile, plane):
@@ -500,8 +510,10 @@
 
     through_n = through_down(ids_row, me, table, rg_all)
     through = [through_n[0]]
-    through += [shift(through_n[k], "g", plane, plane - k) for k in range(1, plane)]
-    input_grad = input_gradient(me, cots, base_weight, through)
+    for k in range(1, plane):
+        through.append(shift(through_n[k], "g", plane, plane - k))
+    base_grad = base_gradient(me, cots, base_weight)
+    input_grad = input_gradient(me, base_grad, through)
 
     output, up_send = output_and_up(ids, ranks, slots, cotangent, frozen, owned)
     up_got = exchange(up_send)

time: 272 us -> 272 us (level)
  waiting for transfers between devices: 64 us -> 57.6 us
  Pallas kernels: 47.2 us -> 50.6 us
  starting transfers between devices: 101 us -> 104 us
    ppermute x47, waiting for transfers between devices: 36 us -> 29.6 us  [shift(): return lax.ppermute(x, axis, [(i, (i + k) % size) for i in range(size)])]
    pallas_call x1 -> x2, Pallas kernels: 9.87 us -> 13.3 us  [the longest x1 8.79 us: base_gradient(): pl.pallas_call(kernel, grid=(features // tile,), in_specs=[SMEM()] + [pl....]
    ppermute x47, starting transfers between devices: 72.2 us -> 75.2 us  [shift(): return lax.ppermute(x, axis, [(i, (i + k) % size) for i in range(size)])]
  transfers between devices with their start and end apart: 53 -> 53, of which waited for: 20 -> 17; matrix products, arithmetic and copies ran while one was open for 6% -> 6% of each run, Pallas kernels for 15% -> 17%
where the time goes in v3:
time: 272 us; the launch traced here: 268 us
  starting transfers between devices  104 us (38%)
  waiting for transfers between devices  57.6 us (21%)
  Pallas kernels  50.6 us (19%)
  blocking collectives  18 us (7%)
  between operations  14.5 us (5%)
  local copies, waits for them, and re-layouts  11.3 us (4%)
  other arithmetic  6.07 us (2%)
  matrix products  5.84 us (2%)
    ppermute x47, starting transfers between devices, shift(): return lax.ppermute(x, axis, [(i, (i + k) % size) for i in range(size)])  75.2 us
    ppermute x47, waiting for transfers between devices, shift(): return lax.ppermute(x, axis, [(i, (i + k) % size) for i in range(size)])  29.6 us
    all_to_all x4, starting transfers between devices, exchange(): return lax.all_to_all(x, axis, split_axis=0, concat_axis=0, tiled=True)  28.5 us
    all_to_all x4, waiting for transfers between devices, exchange(): return lax.all_to_all(x, axis, split_axis=0, concat_axis=0, tiled=True)  27.9 us
    all_to_all x1, blocking collectives, exchange(): return lax.all_to_all(x, axis, split_axis=0, concat_axis=0, tiled=True)  18 us
    pallas_call x1, Pallas kernels, base_gradient(): pl.pallas_call(kernel, grid=(features // tile,), in_specs=[SMEM()] + [pl....  8.79 us
    pallas_call x1, Pallas kernels, down_terms(): pl.pallas_call(kernel, in_specs=[SMEM(), SMEM()] + [HBM()] * (2 * plane),...  6.65 us
    pallas_call x1, Pallas kernels, through_down(): pl.pallas_call(kernel, in_specs=[SMEM(), SMEM(), VMEM()] + [HBM()] * plan...  6.23 us
  transfers between devices with their start and end apart: 53, of which 17 were waited for; matrix products, arithmetic and copies ran while one was open for 6% of the time, Pallas kernels for 17%

profile of v3, /device:TPU:37, one launch (start us, length us, event | category | flops | bytes accessed | tf_op | source)
XLA Modules:
  0.0 267.6 jit_solution(1536827364839149288)
XLA Ops:
  27.1 8.0 %all-to-all-start.1 = ((bf16[8,4,32,256]{3,2,1,0:T(8,128)(2,1)}), bf16[8,4,32,256]{3,2,1,0:T(8,128)(2,1)S(1)}, u32[]{:S(2)}, u32[]{:S(2)}) async-start(bf16[8,4,32,256]{3,2,1,0:T(8,128)(2,1)} %broadcast_in_dim.10), calls=%async_computation.1 | async-start | bytes 1048576 | tf_op jit(solution)/shard_map/all_to_all | solution.py:456
  35.7 17.1 %all-to-all-done.1.all_ref = bf16[8,4,32,256]{3,2,1,0:T(8,128)(2,1)S(1)} async-done(((bf16[8,4,32,256]{3,2,1,0:T(8,128)(2,1)}), bf16[8,4,32,256]{3,2,1,0:T(8,128)(2,1)S(1)}, u32[]{:S(2)}, u32[]{:S(2)}) %all-to-all-start.1) | async-done | bytes 524320 | tf_op jit(solution)/shard_map/all_to_all | solution.py:456
  53.6 3.7 %select_up.1 = bf16[8,8,32,256]{3,2,1,0:T(8,128)(2,1)} custom-call(s32[128]{0:T(128)} %reshape.22.ids_ref, s32[3]{0:T(128)} %pad_add_fusion.me_ref, bf16[8,4,32,256]{3,2,1,0:T(8,128)(2,1)} %copy-done.3), custom_call_target="tpu_custom_call" | custom-call | tf_op jit(solution)/shard_map/select_up/pallas_call | solution.py:99
  57.3 9.0 %all-to-all-start.2 = ((bf16[8,8,32,256]{3,2,1,0:T(8,128)(2,1)}), bf16[8,8,32,256]{3,2,1,0:T(8,128)(2,1)S(1)}, u32[]{:S(2)}, u32[]{:S(2)}) async-start(bf16[8,8,32,256]{3,2,1,0:T(8,128)(2,1)} %select_up.1), calls=%async_computation.2 | async-start | bytes 2097152 | tf_op jit(solution)/shard_map/all_to_all | solution.py:456
  68.4 10.6 %all-to-all-done.2.slots_ref = bf16[8,8,32,256]{3,2,1,0:T(8,128)(2,1)S(1)} async-done(((bf16[8,8,32,256]{3,2,1,0:T(8,128)(2,1)}), bf16[8,8,32,256]{3,2,1,0:T(8,128)(2,1)S(1)}, u32[]{:S(2)}, u32[]{:S(2)}) %all-to-all-start.2) | async-done | bytes 1048608 | tf_op jit(solution)/shard_map/all_to_all | solution.py:456
  82.1 2.9 %collective-permute-start.25 = (f32[4,32,128]{2,1,0:T(8,128)}, f32[4,32,128]{2,1,0:T(8,128)S(1)}, u32[]{:S(2)}, u32[]{:S(2)}) collective-permute-start(f32[4,32,128]{2,1,0:T(8,128)} %rank_grad_part.1), channel_id=1, source_target_pairs={{0,3},{1,0},{2,1},{3,2},{4,7},{5,4},{6,5},{7,6},{8,11},{9,8},{10,9... | collective-permute-start | bytes 196616 | tf_op jit(solution)/shard_map/ppermute | solution.py:441
  85.9 3.9 %collective-permute-start.11 = (bf16[512,256]{1,0:T(8,128)(2,1)}, bf16[512,256]{1,0:T(8,128)(2,1)S(1)}, u32[]{:S(2)}, u32[]{:S(2)}) collective-permute-start(bf16[512,256]{1,0:T(8,128)(2,1)} %get-tuple-element.49), channel_id=1, source_target_pairs={{0,20},{4,24},{8,28},{12,0},{16,4},{20,8},{24,12},{28,16},{1,21},{... | collective-permute-start | bytes 786440 | tf_op jit(solution)/shard_map/ppermute | solution.py:441
  96.6 8.5 %collective-permute-done.11.refs_5_.refs_13_ = bf16[512,256]{1,0:T(8,128)(2,1)S(1)} collective-permute-done((bf16[512,256]{1,0:T(8,128)(2,1)}, bf16[512,256]{1,0:T(8,128)(2,1)S(1)}, u32[]{:S(2)}, u32[]{:S(2)}) %collective-permute-start.11) | collective-permute-done | bytes 262176 | tf_op jit(solution)/shard_map/ppermute | solution.py:441
  112.6 5.5 %collective-permute-start.28 = (bf16[4,32,128]{2,1,0:T(8,128)(2,1)S(1)}, bf16[4,32,128]{2,1,0:T(8,128)(2,1)S(1)}, u32[]{:S(2)}, u32[]{:S(2)}) collective-permute-start(bf16[4,32,128]{2,1,0:T(8,128)(2,1)S(1)} %multiply_convert_fusion.refs_0_), channel_id=1, source_target_pairs={{0,12},{4,16},{8,20},{12,24},{16,28},{20,0},{24,4},{28,8},{1,13},{... | collective-permute-start | bytes 98312 | tf_op jit(solution)/shard_map/ppermute | solution.py:441
  122.6 6.6 %down_terms.1 = bf16[256,32,256]{2,1,0:T(8,128)(2,1)} custom-call(s32[128]{0:T(128)} %reshape.22.ids_ref, s32[3]{0:T(128)} %pad_add_fusion.me_ref, bf16[4,32,128]{2,1,0:T(8,128)(2,1)} %copy-done.10, bf16[4,32,128]{2,1,0:T(8,128)(2,1)} %copy-done.27, bf16[4,32,128]{2,1,0:T(8,128)(2,1)} %copy-done.26, bf16[4,32,128]{2,1,0:T(8,128)(2,1)} %copy-done.25, ...), custom_call_target="tpu_custom_call" | custom-call | tf_op jit(solution)/shard_map/down_terms/pallas_call | solution.py:178
  129.3 5.8 %fusion.5 = f32[512,1024]{1,0:T(8,128)} fusion(bf16[512,2048]{1,0:T(8,128)(2,1)S(1)} %copy-done.2, bf16[2048,1024]{1,0:T(8,128)(2,1)} %refs_4_.1), kind=kOutput, calls=%fused_computation.43 | convolution fusion | flops 2147483648 | bytes 8388608 | tf_op jit(solution)/shard_map/dot_general | solution.py:482
  135.7 6.0 %rank_part.1 = bf16[8,4,32,128]{3,2,1,0:T(8,128)(2,1)} custom-call(s32[128]{0:T(128)} %fusion.ids_ref, s32[3]{0:T(128)} %pad_add_fusion.me_ref, bf16[256,32,256]{2,1,0:T(8,128)(2,1)} %all-gather.2.cloned.1.call-done.table_ref, bf16[512,256]{1,0:T(8,128)(2,1)} %get-tuple-element.54.refs_0_.refs_8_, bf16[512,256]{1,0:T(8,128)(2,1)} %collective-permute-done.7.refs_1_.refs_9_, ...), custom_call_target="tpu_custom_call" | custom-call | tf_op jit(solution)/shard_map/rank_part/pallas_call | solution.py:219
  141.7 6.2 %all-to-all-start = ((bf16[8,4,32,128]{3,2,1,0:T(8,128)(2,1)}), bf16[8,4,32,128]{3,2,1,0:T(8,128)(2,1)S(1)}, u32[]{:S(2)}, u32[]{:S(2)}) async-start(bf16[8,4,32,128]{3,2,1,0:T(8,128)(2,1)} %rank_part.1), calls=%async_computation | async-start | bytes 524288 | tf_op jit(solution)/shard_map/all_to_all | solution.py:456
  157.2 6.0 %collective-permute-done.18 = bf16[512,256]{1,0:T(8,128)(2,1)} collective-permute-done((bf16[512,256]{1,0:T(8,128)(2,1)S(1)}, bf16[512,256]{1,0:T(8,128)(2,1)}, u32[]{:S(2)}, u32[]{:S(2)}) %collective-permute-start.18) | collective-permute-done | bytes 262176 | tf_op jit(solution)/shard_map/ppermute | solution.py:441
  170.1 18.0 %all_to_all.25.got_ref = bf16[8,8,32,256]{3,2,1,0:T(8,128)(2,1)} all-to-all(bf16[8,8,32,256]{3,2,1,0:T(8,128)(2,1)} %get-tuple-element.43), channel_id=1, replica_groups=mesh['z'=8,'g'=8,'mp'=4] {'g'}, dimensions={0} | all-to-all | bytes 2097152 | tf_op jit(solution)/shard_map/all_to_all | solution.py:456
  188.1 3.8 %gather_up.1 = bf16[8,4,32,256]{3,2,1,0:T(8,128)(2,1)} custom-call(s32[128]{0:T(128)} %reshape.22.ids_ref, s32[3]{0:T(128)} %pad_add_fusion.me_ref, bf16[8,8,32,256]{3,2,1,0:T(8,128)(2,1)} %all_to_all.25.got_ref), custom_call_target="tpu_custom_call" | custom-call | tf_op jit(solution)/shard_map/gather_up/pallas_call | solution.py:319
  191.9 5.3 %all-to-all-start.4 = ((bf16[8,4,32,256]{3,2,1,0:T(8,128)(2,1)}), bf16[8,4,32,256]{3,2,1,0:T(8,128)(2,1)S(1)}, u32[]{:S(2)}, u32[]{:S(2)}) async-start(bf16[8,4,32,256]{3,2,1,0:T(8,128)(2,1)} %gather_up.1), calls=%async_computation.5 | async-start | bytes 1048576 | tf_op jit(solution)/shard_map/all_to_all | solution.py:456
  200.7 6.2 %through_down.1 = (bf16[512,256]{1,0:T(8,128)(2,1)}, bf16[512,256]{1,0:T(8,128)(2,1)}, bf16[512,256]{1,0:T(8,128)(2,1)}, bf16[512,256]{1,0:T(8,128)(2,1)}, bf16[...) custom-call(s32[128]{0:T(128)} %fusion.ids_ref, ...), custom_call_target="tpu_custom_call" | custom-call | tf_op jit(solution)/shard_map/through_down/pallas_call | solution.py:257
  210.3 3.2 %collective-permute-start.35 = (bf16[512,256]{1,0:T(8,128)(2,1)}, bf16[512,256]{1,0:T(8,128)(2,1)S(1)}, u32[]{:S(2)}, u32[]{:S(2)}) collective-permute-start(bf16[512,256]{1,0:T(8,128)(2,1)} %get-tuple-element.38), channel_id=1, source_target_pairs={{0,20},{4,24},{8,28},{12,0},{16,4},{20,8},{24,12},{28,16},{1,21},{... | collective-permute-start | bytes 786440 | tf_op jit(solution)/shard_map/ppermute | solution.py:441
  218.8 5.8 %collective-permute-start.39 = (bf16[512,256]{1,0:T(8,128)(2,1)}, bf16[512,256]{1,0:T(8,128)(2,1)S(1)}, u32[]{:S(2)}, u32[]{:S(2)}) collective-permute-start(bf16[512,256]{1,0:T(8,128)(2,1)} %get-tuple-element.42), channel_id=1, source_target_pairs={{0,4},{4,8},{8,12},{12,16},{16,20},{20,24},{24,28},{28,0},{1,5},{5... | collective-permute-start | bytes 786440 | tf_op jit(solution)/shard_map/ppermute | solution.py:441
  226.4 3.6 %collective-permute-start.45 = (bf16[4,32,256]{2,1,0:T(8,128)(2,1)}, bf16[4,32,256]{2,1,0:T(8,128)(2,1)}, u32[]{:S(2)}, u32[]{:S(2)}) collective-permute-start(bf16[4,32,256]{2,1,0:T(8,128)(2,1)} %get-tuple-element.56), channel_id=1, source_target_pairs={{0,24},{4,28},{8,0},{12,4},{16,8},{20,12},{24,16},{28,20},{1,25},{... | collective-permute-start | bytes 196616 | tf_op jit(solution)/shard_map/ppermute | solution.py:441
  230.0 8.8 %base_gradient.1.base_ref = f32[512,2048]{1,0:T(8,128)} custom-call(s32[3]{0:T(128)} %pad_add_fusion.me_ref, bf16[512,256]{1,0:T(8,128)(2,1)} %cot_ref.3, bf16[512,256]{1,0:T(8,128)(2,1)} %copy-done.13, bf16[512,256]{1,0:T(8,128)(2,1)} %copy-done.12, bf16[512,256]{1,0:T(8,128)(2,1)} %copy-done.11, bf16[2048,1024]{1,0:T(8,128)(2,1)} %refs_4_.1), custom_call_target="tpu_custom_call" | custom-call | tf_op jit(solution)/shard_map/base_gradient/pallas_call | solution.py:346
  239.7 4.5 %input_gradient.1 = bf16[512,2048]{1,0:T(8,128)(2,1)} custom-call(s32[3]{0:T(128)} %pad_add_fusion.me_ref, f32[512,2048]{1,0:T(8,128)} %base_gradient.1.base_ref, bf16[512,256]{1,0:T(8,128)(2,1)} %get-tuple-element.35.refs_0_, bf16[512,256]{1,0:T(8,128)(2,1)} %copy-done.14, bf16[512,256]{1,0:T(8,128)(2,1)} %copy-done.15, bf16[512,256]{1,0:T(8,128)(2,1)} %copy-done.16, ...), custom_call_target="tpu_custom_call" | custom-call | tf_op jit(solution)/shard_map/input_gradient/pallas_call | solution.py:370
  244.2 5.9 %collective-permute-start.44 = (bf16[4,32,256]{2,1,0:T(8,128)(2,1)S(1)}, bf16[4,32,256]{2,1,0:T(8,128)(2,1)S(1)}, u32[]{:S(2)}, u32[]{:S(2)}) collective-permute-start(bf16[4,32,256]{2,1,0:T(8,128)(2,1)S(1)} %get-tuple-element.57), channel_id=1, source_target_pairs={{0,20},{4,24},{8,28},{12,0},{16,4},{20,8},{24,12},{28,16},{1,21},{... | collective-permute-start | bytes 196616 | tf_op jit(solution)/shard_map/ppermute | solution.py:441
  (198 shorter events, 88.2 us)
Async XLA Ops:
  7.2 128.6 %all-gather.2.cloned.1.call-start = ((), (), s32[]{:S(2)}) async-start(), calls=%async_computation.6 | async-start | bytes 4718592 | tf_op jit(solution)/shard_map/all_gather | solution.py:471
  27.1 25.8 %all-to-all-start.1 = ((bf16[8,4,32,256]{3,2,1,0:T(8,128)(2,1)}), bf16[8,4,32,256]{3,2,1,0:T(8,128)(2,1)S(1)}, u32[]{:S(2)}, u32[]{:S(2)}) async-start(bf16[8,4,32,256]{3,2,1,0:T(8,128)(2,1)} %broadcast_in_dim.10), calls=%async_computation.1 | async-start | bytes 1048576 | tf_op jit(solution)/shard_map/all_to_all | solution.py:456
  57.3 21.6 %all-to-all-start.2 = ((bf16[8,8,32,256]{3,2,1,0:T(8,128)(2,1)}), bf16[8,8,32,256]{3,2,1,0:T(8,128)(2,1)S(1)}, u32[]{:S(2)}, u32[]{:S(2)}) async-start(bf16[8,8,32,256]{3,2,1,0:T(8,128)(2,1)} %select_up.1), calls=%async_computation.2 | async-start | bytes 2097152 | tf_op jit(solution)/shard_map/all_to_all | solution.py:456
  66.3 158.3 %reduce-scatter.2.cloned.1.call-start = ((), (), s32[]{:S(2)}) async-start(), calls=%async_computation.7 | async-start | bytes 4718592 | tf_op jit(solution)/shard_map/reduce_scatter | solution.py:501
  67.7 18.2 %collective-permute-start.13 = (bf16[512,256]{1,0:T(8,128)(2,1)}, bf16[512,256]{1,0:T(8,128)(2,1)S(1)}, u32[]{:S(2)}, u32[]{:S(2)}) collective-permute-start(bf16[512,256]{1,0:T(8,128)(2,1)} %get-tuple-element.47), channel_id=1, source_target_pairs={{0,28},{4,0},{8,4},{12,8},{16,12},{20,16},{24,20},{28,24},{1,29},{... | collective-permute-start | bytes 786440 | tf_op jit(solution)/shard_map/ppermute | solution.py:441
  68.1 21.7 %collective-permute-start.12 = (bf16[512,256]{1,0:T(8,128)(2,1)}, bf16[512,256]{1,0:T(8,128)(2,1)}, u32[]{:S(2)}, u32[]{:S(2)}) collective-permute-start(bf16[512,256]{1,0:T(8,128)(2,1)} %get-tuple-element.48), channel_id=1, source_target_pairs={{0,24},{4,28},{8,0},{12,4},{16,8},{20,12},{24,16},{28,20},{1,25},{... | collective-permute-start | bytes 786440 | tf_op jit(solution)/shard_map/ppermute | solution.py:441
  85.9 19.1 %collective-permute-start.11 = (bf16[512,256]{1,0:T(8,128)(2,1)}, bf16[512,256]{1,0:T(8,128)(2,1)S(1)}, u32[]{:S(2)}, u32[]{:S(2)}) collective-permute-start(bf16[512,256]{1,0:T(8,128)(2,1)} %get-tuple-element.49), channel_id=1, source_target_pairs={{0,20},{4,24},{8,28},{12,0},{16,4},{20,8},{24,12},{28,16},{1,21},{... | collective-permute-start | bytes 786440 | tf_op jit(solution)/shard_map/ppermute | solution.py:441
  89.8 15.2 %collective-permute-start.10 = (bf16[512,256]{1,0:T(8,128)(2,1)}, bf16[512,256]{1,0:T(8,128)(2,1)S(1)}, u32[]{:S(2)}, u32[]{:S(2)}) collective-permute-start(bf16[512,256]{1,0:T(8,128)(2,1)} %get-tuple-element.50), channel_id=1, source_target_pairs={{0,16},{4,20},{8,24},{12,28},{16,0},{20,4},{24,8},{28,12},{1,17},{... | collective-permute-start | bytes 786440 | tf_op jit(solution)/shard_map/ppermute | solution.py:441
  91.6 17.2 %collective-permute-start.9 = (bf16[512,256]{1,0:T(8,128)(2,1)}, bf16[512,256]{1,0:T(8,128)(2,1)S(1)}, u32[]{:S(2)}, u32[]{:S(2)}) collective-permute-start(bf16[512,256]{1,0:T(8,128)(2,1)} %get-tuple-element.51), channel_id=1, source_target_pairs={{0,12},{4,16},{8,20},{12,24},{16,28},{20,0},{24,4},{28,8},{1,13},{... | collective-permute-start | bytes 786440 | tf_op jit(solution)/shard_map/ppermute | solution.py:441
  92.0 17.3 %collective-permute-start.8 = (bf16[512,256]{1,0:T(8,128)(2,1)}, bf16[512,256]{1,0:T(8,128)(2,1)S(1)}, u32[]{:S(2)}, u32[]{:S(2)}) collective-permute-start(bf16[512,256]{1,0:T(8,128)(2,1)} %get-tuple-element.52), channel_id=1, source_target_pairs={{0,8},{4,12},{8,16},{12,20},{16,24},{20,28},{24,0},{28,4},{1,9},{5... | collective-permute-start | bytes 786440 | tf_op jit(solution)/shard_map/ppermute | solution.py:441
  93.2 19.5 %collective-permute-start.7 = (bf16[512,256]{1,0:T(8,128)(2,1)}, bf16[512,256]{1,0:T(8,128)(2,1)}, u32[]{:S(2)}, u32[]{:S(2)}) collective-permute-start(bf16[512,256]{1,0:T(8,128)(2,1)} %get-tuple-element.53), channel_id=1, source_target_pairs={{0,4},{4,8},{8,12},{12,16},{16,20},{20,24},{24,28},{28,0},{1,5},{5... | collective-permute-start | bytes 786440 | tf_op jit(solution)/shard_map/ppermute | solution.py:441
  105.0 13.2 %collective-permute-start.32 = (bf16[4,32,128]{2,1,0:T(8,128)(2,1)S(1)}, bf16[4,32,128]{2,1,0:T(8,128)(2,1)S(1)}, u32[]{:S(2)}, u32[]{:S(2)}) collective-permute-start(bf16[4,32,128]{2,1,0:T(8,128)(2,1)S(1)} %multiply_convert_fusion.refs_0_), channel_id=1, source_target_pairs={{0,28},{4,0},{8,4},{12,8},{16,12},{20,16},{24,20},{28,24},{1,29},{... | collective-permute-start | bytes 98312 | tf_op jit(solution)/shard_map/ppermute | solution.py:441
  105.0 13.2 %collective-permute-start.31 = (bf16[4,32,128]{2,1,0:T(8,128)(2,1)S(1)}, bf16[4,32,128]{2,1,0:T(8,128)(2,1)S(1)}, u32[]{:S(2)}, u32[]{:S(2)}) collective-permute-start(bf16[4,32,128]{2,1,0:T(8,128)(2,1)S(1)} %multiply_convert_fusion.refs_0_), channel_id=1, source_target_pairs={{0,24},{4,28},{8,0},{12,4},{16,8},{20,12},{24,16},{28,20},{1,25},{... | collective-permute-start | bytes 98312 | tf_op jit(solution)/shard_map/ppermute | solution.py:441
  152.1 13.1 %collective-permute-start.16 = (f32[4,32,128]{2,1,0:T(8,128)S(1)}, f32[4,32,128]{2,1,0:T(8,128)S(1)}, u32[]{:S(2)}, u32[]{:S(2)}) collective-permute-start(f32[4,32,128]{2,1,0:T(8,128)S(1)} %convert_reduce_fusion.1), channel_id=1, source_target_pairs={{0,3},{1,0},{2,1},{3,2},{4,7},{5,4},{6,5},{7,6},{8,11},{9,8},{10,9... | collective-permute-start | bytes 196616 | tf_op jit(solution)/shard_map/ppermute | solution.py:441
  191.9 63.7 %all-to-all-start.4 = ((bf16[8,4,32,256]{3,2,1,0:T(8,128)(2,1)}), bf16[8,4,32,256]{3,2,1,0:T(8,128)(2,1)S(1)}, u32[]{:S(2)}, u32[]{:S(2)}) async-start(bf16[8,4,32,256]{3,2,1,0:T(8,128)(2,1)} %gather_up.1), calls=%async_computation.5 | async-start | bytes 1048576 | tf_op jit(solution)/shard_map/all_to_all | solution.py:456
  197.2 13.1 %collective-permute-start.22 = (bf16[512,256]{1,0:T(8,128)(2,1)S(1)}, bf16[512,256]{1,0:T(8,128)(2,1)S(1)}, u32[]{:S(2)}, u32[]{:S(2)}) collective-permute-start(bf16[512,256]{1,0:T(8,128)(2,1)S(1)} %copy-done.1), channel_id=1, source_target_pairs={{0,3},{1,0},{2,1},{3,2},{4,7},{5,4},{6,5},{7,6},{8,11},{9,8},{10,9... | collective-permute-start | bytes 786440 | tf_op jit(solution)/shard_map/ppermute | solution.py:441
  200.0 13.5 %collective-permute-start.21 = (bf16[512,256]{1,0:T(8,128)(2,1)S(1)}, bf16[512,256]{1,0:T(8,128)(2,1)S(1)}, u32[]{:S(2)}, u32[]{:S(2)}) collective-permute-start(bf16[512,256]{1,0:T(8,128)(2,1)S(1)} %copy-done.1), channel_id=1, source_target_pairs={{0,2},{1,3},{2,0},{3,1},{4,6},{5,7},{6,4},{7,5},{8,10},{9,11},{10,... | collective-permute-start | bytes 786440 | tf_op jit(solution)/shard_map/ppermute | solution.py:441
  200.1 15.1 %collective-permute-start.20 = (bf16[512,256]{1,0:T(8,128)(2,1)S(1)}, bf16[512,256]{1,0:T(8,128)(2,1)S(1)}, u32[]{:S(2)}, u32[]{:S(2)}) collective-permute-start(bf16[512,256]{1,0:T(8,128)(2,1)S(1)} %copy-done.1), channel_id=1, source_target_pairs={{0,1},{1,2},{2,3},{3,0},{4,5},{5,6},{6,7},{7,4},{8,9},{9,10},{10,1... | collective-permute-start | bytes 786440 | tf_op jit(solution)/shard_map/ppermute | solution.py:441
  210.3 16.1 %collective-permute-start.35 = (bf16[512,256]{1,0:T(8,128)(2,1)}, bf16[512,256]{1,0:T(8,128)(2,1)S(1)}, u32[]{:S(2)}, u32[]{:S(2)}) collective-permute-start(bf16[512,256]{1,0:T(8,128)(2,1)} %get-tuple-element.38), channel_id=1, source_target_pairs={{0,20},{4,24},{8,28},{12,0},{16,4},{20,8},{24,12},{28,16},{1,21},{... | collective-permute-start | bytes 786440 | tf_op jit(solution)/shard_map/ppermute | solution.py:441
  215.3 23.5 %collective-permute-start.37 = (bf16[512,256]{1,0:T(8,128)(2,1)}, bf16[512,256]{1,0:T(8,128)(2,1)S(1)}, u32[]{:S(2)}, u32[]{:S(2)}) collective-permute-start(bf16[512,256]{1,0:T(8,128)(2,1)} %get-tuple-element.40), channel_id=1, source_target_pairs={{0,12},{4,16},{8,20},{12,24},{16,28},{20,0},{24,4},{28,8},{1,13},{... | collective-permute-start | bytes 786440 | tf_op jit(solution)/shard_map/ppermute | solution.py:441
  218.0 20.9 %collective-permute-start.38 = (bf16[512,256]{1,0:T(8,128)(2,1)}, bf16[512,256]{1,0:T(8,128)(2,1)S(1)}, u32[]{:S(2)}, u32[]{:S(2)}) collective-permute-start(bf16[512,256]{1,0:T(8,128)(2,1)} %get-tuple-element.41), channel_id=1, source_target_pairs={{0,8},{4,12},{8,16},{12,20},{16,24},{20,28},{24,0},{28,4},{1,9},{5... | collective-permute-start | bytes 786440 | tf_op jit(solution)/shard_map/ppermute | solution.py:441
  218.8 20.0 %collective-permute-start.39 = (bf16[512,256]{1,0:T(8,128)(2,1)}, bf16[512,256]{1,0:T(8,128)(2,1)S(1)}, u32[]{:S(2)}, u32[]{:S(2)}) collective-permute-start(bf16[512,256]{1,0:T(8,128)(2,1)} %get-tuple-element.42), channel_id=1, source_target_pairs={{0,4},{4,8},{8,12},{12,16},{16,20},{20,24},{24,28},{28,0},{1,5},{5... | collective-permute-start | bytes 786440 | tf_op jit(solution)/shard_map/ppermute | solution.py:441
  226.4 27.2 %collective-permute-start.46 = (bf16[4,32,256]{2,1,0:T(8,128)(2,1)}, bf16[4,32,256]{2,1,0:T(8,128)(2,1)S(1)}, u32[]{:S(2)}, u32[]{:S(2)}) collective-permute-start(bf16[4,32,256]{2,1,0:T(8,128)(2,1)} %get-tuple-element.55), channel_id=1, source_target_pairs={{0,28},{4,0},{8,4},{12,8},{16,12},{20,16},{24,20},{28,24},{1,29},{... | collective-permute-start | bytes 196616 | tf_op jit(solution)/shard_map/ppermute | solution.py:441
  226.4 27.7 %collective-permute-start.45 = (bf16[4,32,256]{2,1,0:T(8,128)(2,1)}, bf16[4,32,256]{2,1,0:T(8,128)(2,1)}, u32[]{:S(2)}, u32[]{:S(2)}) collective-permute-start(bf16[4,32,256]{2,1,0:T(8,128)(2,1)} %get-tuple-element.56), channel_id=1, source_target_pairs={{0,24},{4,28},{8,0},{12,4},{16,8},{20,12},{24,16},{28,20},{1,25},{... | collective-permute-start | bytes 196616 | tf_op jit(solution)/shard_map/ppermute | solution.py:441
  (72 other events, 602.4 us)
Sparse Core Ops, SparseCore 0:
  25.5 63.1 all-gather.1
  129.4 50.8 reduce-scatter.1
